TPU v7x, 32 devices: a whole 2x2x4 slice. The times are simulated.
32 devices in a mesh: fsdp: 8 (over z, y), dp: 4 (over x, core).
Axes of the slice: x: 2, y: 2, z: 4, core: 2. Of those that a mesh axis runs over, the one named last changes fastest.
Arguments:
- byte_ids: int32 [64, 1024], P(('fsdp', 'dp')), may hold values from 0 to 255
- doc_lengths: int32 [64, 8], P(('fsdp', 'dp')), may hold values from 1 to 512, 1024 in all within a row
- pad_mask: int32 [64, 1024], P(('fsdp', 'dp')), may hold values from 0 to 1, as said below
- embedding: bfloat16 [256, 768], P(None, 'fsdp'), may hold values from -6 to 6
- conv_weight: bfloat16 [5, 768, 768], P(None, 'fsdp'), may hold values from -0.09375 to 0.09375
- conv_bias: bfloat16 [768], P('fsdp'), may hold values from -3 to 3
- scorer: bfloat16 [768], P('fsdp'), may hold values from -0.3125 to 0.3125
- cotangent: bfloat16 [64, 512, 768], P(('fsdp', 'dp')), may hold values from -6 to 6
- aux_weight: float32 [], replicated, may hold values from 8192 to 16384
Outputs:
- blocks: bfloat16 [64, 512, 768], P(('fsdp', 'dp'))
- loss: float32 [], replicated
- emb_grad: float32 [256, 768], P(None, 'fsdp')
- conv_grad: float32 [5, 768, 768], P(None, 'fsdp')
- bias_grad: float32 [768], P('fsdp')
- score_grad: float32 [768], P('fsdp')
Inputs may be any that keep to these rules, and one draw needn't show every extreme that they name: `doc_lengths`: each row's 8 document lengths sum to 1024; the longest document of a row is 512 long. `pad_mask`: in every row the real bytes come first and padding follows; every row holds 256 or more real bytes.
All inputs are finite; a program needn't handle non-finite values.
Results may differ from a plain program's by a relative error of at most 0.0046.
Values may be sent and summed in bfloat16 or wider, within the bound.
A program may use at most 320 MiB of HBM per device.

v0:
```python
import jax
import jax.numpy as jnp
from jax import lax
from jax.sharding import PartitionSpec as P

TAPS = 5
SIZES = 4


def segment_ids(length_row, length):
    ends = jnp.cumsum(length_row, axis=-1)
    places = jnp.arange(length, dtype=jnp.int32)
    return jnp.sum((places[:, None] >= ends[None, :]).astype(jnp.int32), axis=1)


def partner_same(segment, offset):
    length = segment.shape[-1]
    places = jnp.arange(length, dtype=jnp.int32)
    inside = (places + offset >= 0) & (places + offset < length)
    return inside & (jnp.roll(segment, -offset, axis=-1) == segment)


def latent_row(hidden, scorer_input_rows, segment, real_mask):
    length = hidden.shape[0]
    places = jnp.arange(length, dtype=jnp.int32)
    mean_list = []
    for block_size in range(1, SIZES + 1):
        member_sum = jnp.zeros_like(hidden)
        member_count = jnp.zeros((length,), jnp.float32)
        for offset in range(1 - block_size, block_size):
            member = partner_same(segment, offset) & (
                (places + offset) // block_size == places // block_size
            )
            weight_here = member.astype(jnp.float32) * jnp.roll(real_mask, -offset)
            member_sum = member_sum + jnp.roll(hidden, -offset, axis=0) * weight_here[:, None]
            member_count = member_count + weight_here
        mean_list.append(member_sum / jnp.maximum(member_count, 1.0)[:, None])
    block_average_values = jnp.stack(mean_list)
    block_score_rows = jnp.einsum(
        "agn,n->ga", block_average_values, scorer_input_rows, precision=lax.Precision.HIGHEST
    )
    similar = jnp.dot(block_score_rows, block_score_rows.T, precision=lax.Precision.HIGHEST)
    allowed = (segment[:, None] == segment[None, :]) & (real_mask[None, :] > 0.5) | (
        places[:, None] == places[None, :]
    )
    similar = jnp.where(allowed, similar, -1000000000.0)
    top_similar = jnp.max(similar, axis=1, keepdims=True)
    power_term = jnp.exp(similar - top_similar)
    attention = power_term / jnp.sum(power_term, axis=1, keepdims=True)
    calibrated = jnp.dot(attention, block_score_rows, precision=lax.Precision.HIGHEST)
    log_weight = jax.nn.log_softmax(calibrated, axis=1)
    block_size_weight = jnp.exp(log_weight)
    entropy = -jnp.sum(block_size_weight * log_weight, axis=1)
    hidden_state_rows = jnp.einsum(
        "ue,euh->uh", block_size_weight, block_average_values, precision=lax.Precision.HIGHEST
    )
    uneven_location = places % 2 == 1
    pair_weight = real_mask * jnp.where(
        uneven_location, jnp.roll(segment, 1) == segment, True
    ).astype(jnp.float32)
    pooled = (hidden_state_rows * pair_weight[:, None]).reshape(length // 2, 2, -1).sum(axis=1)
    pair_count = pair_weight.reshape(length // 2, 2).sum(axis=1)
    return (pooled / jnp.maximum(pair_count, 1.0)[:, None], jnp.sum(real_mask * entropy))


def shards(
    byte_ids,
    doc_lengths,
    pad_mask,
    embedding,
    conv_weight,
    conv_bias,
    scorer,
    cotangent,
    aux_weight,
):
    emb_full, conv_full, bias_full, score_full = (
        lax.all_gather(embedding, "fsdp", axis=1, tiled=True),
        lax.all_gather(conv_weight, "fsdp", axis=1, tiled=True),
        lax.all_gather(conv_bias, "fsdp", axis=0, tiled=True),
        lax.all_gather(scorer, "fsdp", axis=0, tiled=True),
    )
    rows_here, length = byte_ids.shape
    vocab_size, model_width = emb_full.shape
    real_mask = pad_mask.astype(jnp.float32)
    segment = jax.vmap(segment_ids, in_axes=(0, None))(doc_lengths, length)
    count_here = jnp.sum(real_mask)
    total_count = lax.psum(count_here, ("fsdp", "dp"))
    byte_table = (byte_ids[:, :, None] == jnp.arange(vocab_size, dtype=jnp.int32)).astype(
        jnp.bfloat16
    )
    looked_up = jnp.einsum("rlv,vd->rld", byte_table, emb_full, preferred_element_type=jnp.float32)
    inputs = (looked_up * real_mask[:, :, None]).astype(jnp.bfloat16)
    keep_list = []
    tap_list = []
    for tap_index in range(TAPS):
        offset = tap_index - TAPS // 2
        keep = partner_same(segment, offset).astype(jnp.bfloat16)
        keep_list.append(keep)
        tap_list.append(jnp.roll(inputs, -offset, axis=1) * keep[:, :, None])
    stacked = jnp.concatenate(tap_list, axis=2)
    conv_matrix = conv_full.reshape(TAPS * model_width, model_width)
    hidden = jnp.einsum(
        "rlc,cd->rld", stacked, conv_matrix, preferred_element_type=jnp.float32
    ) + bias_full.astype(jnp.float32)

    def local_piece(hidden_in, scorer_input_rows):
        pooled_rows, entropy_rows = jax.vmap(latent_row, in_axes=(0, None, 0, 0))(
            hidden_in, scorer_input_rows, segment, real_mask
        )
        return (pooled_rows, jnp.sum(entropy_rows))

    (pooled, entropy_here), pullback = jax.vjp(local_piece, hidden, score_full.astype(jnp.float32))
    entropy_total = lax.psum(entropy_here, ("fsdp", "dp"))
    loss = entropy_total / total_count
    hidden_grad, score_grad = pullback((cotangent.astype(jnp.float32), aux_weight / total_count))
    hidden_low = hidden_grad.astype(jnp.bfloat16)
    bias_grad = jnp.sum(hidden_low.astype(jnp.float32), axis=(0, 1))
    conv_grad = jnp.einsum(
        "rlc,rld->cd", stacked, hidden_low, preferred_element_type=jnp.float32
    ).reshape(TAPS, model_width, model_width)
    conv_back = lax.all_gather(conv_weight, "fsdp", axis=1, tiled=True).reshape(
        TAPS * model_width, model_width
    )
    tap_grad = jnp.einsum(
        "rld,cd->rlc", hidden_low, conv_back, preferred_element_type=jnp.float32
    ).reshape(rows_here, length, TAPS, model_width)
    input_grad = jnp.zeros((rows_here, length, model_width), jnp.float32)
    for tap_index in range(TAPS):
        offset = tap_index - TAPS // 2
        masked_grad = (
            tap_grad[:, :, tap_index] * keep_list[tap_index].astype(jnp.float32)[:, :, None]
        )
        input_grad = input_grad + jnp.roll(masked_grad, offset, axis=1)
    input_low = (input_grad * real_mask[:, :, None]).astype(jnp.bfloat16)
    emb_grad = jnp.einsum("rlv,rld->vd", byte_table, input_low, preferred_element_type=jnp.float32)
    grads = (emb_grad, conv_grad, bias_grad, score_grad)
    summed = lax.psum((grads[0], grads[1], grads[2], grads[3]), "dp")
    shares = (
        lax.psum_scatter(summed[0], "fsdp", scatter_dimension=1, tiled=True),
        lax.psum_scatter(summed[1], "fsdp", scatter_dimension=1, tiled=True),
        lax.psum_scatter(summed[2], "fsdp", scatter_dimension=0, tiled=True),
        lax.psum_scatter(summed[3], "fsdp", scatter_dimension=0, tiled=True),
    )
    return (pooled.astype(jnp.bfloat16), loss, shares[0], shares[1], shares[2], shares[3])


def solution(mesh):
    return jax.shard_map(
        shards,
        mesh=mesh,
        in_specs=(
            P(("fsdp", "dp"), None),
            P(("fsdp", "dp"), None),
            P(("fsdp", "dp"), None),
            P(None, "fsdp"),
            P(None, "fsdp", None),
            P("fsdp"),
            P("fsdp"),
            P(("fsdp", "dp"), None, None),
            P(),
        ),
        out_specs=(
            P(("fsdp", "dp"), None, None),
            P(),
            P(None, "fsdp"),
            P(None, "fsdp", None),
            P("fsdp"),
            P("fsdp"),
        ),
        check_vma=False,
    )
```

profile of v0, /device:TPU:1, one launch (start us, length us, event | category | flops | bytes accessed | tf_op | source)
XLA Modules:
  0.0 937.3 jit_solution(10693173568376501567)
XLA Ops:
  11.3 43.4 %psum.43 = f32[]{:T(128)} all-reduce(f32[]{:T(128)} %get-tuple-element.90), channel_id=1, replica_groups=mesh['fsdp'=8,'dp'=4] {'fsdp','dp'}, use_global_device_ids=true, to_apply=%region_12.13 | all-reduce | flops 1 | bytes 8 | tf_op jit(solution)/shard_map/psum | solution.py:88
  58.4 16.8 %all-reduce.31 = (bf16[768]{0:T(1024)(128)(2,1)S(1)}, bf16[768]{0:T(1024)(128)(2,1)S(1)}) all-reduce(bf16[768]{0:T(1024)(128)(2,1)S(1)} %dynamic-update-slice.1, bf16[768]{0:T(1024)(128)(2,1)S(1)} %dynamic-update-slice), channel_id=1, replica_groups=mesh['fsdp'=8,'dp'=4] {'fsdp'}, use_global_device_ids=true, to_apply=%add.25 | all-reduce | flops 1536 | bytes 6144
  79.6 4.7 broadcast_in_dim.28
  84.3 8.6 reshape.1229
  94.3 26.1 %all_gather.13 = bf16[256,768]{0,1:T(8,128)(2,1)S(1)} all-gather(bf16[256,96]{0,1:T(8,128)(2,1)S(1)} %copy-done.30), channel_id=1, replica_groups=mesh['fsdp'=8,'dp'=4] {'fsdp'}, dimensions={1}, use_global_device_ids=true | all-gather | bytes 442368 | tf_op jit(solution)/shard_map/all_gather | solution.py:78
  137.9 3.1 fusion.187
  141.0 3.2 broadcast_multiply_fusion
  144.2 17.7 %broadcast_add_fusion = f32[2,1024,768]{2,1,0:T(8,128)S(1)} fusion(f32[768]{0:T(1024)S(1)} %convert_element_type.147, bf16[2,1024,3840]{2,1,0:T(8,128)(2,1)} %fusion.56, bf16[3840,768,1]{1,0,2:T(8,128)(2,1)} %bitcast.204), kind=kOutput, calls=%fused_computation.109 | convolution fusion | flops 12081168384 | bytes 27921408 | tf_op jit(solution)/shard_map/rlc,cd->rld/dot_general | solution.py:103
  162.0 5.4 fusion.159
  167.4 5.6 fusion.161
  172.9 5.5 fusion.157
  178.4 13.1 %divide_bitcast_fusion.2 = (f32[1,2,1024,768]{3,2,1,0:T(8,128)}, f32[1,2,1024,768]{3,2,1,0:T(8,128)}) fusion(f32[2,1024,768]{2,1,0:T(8,128)S(1)} %broadcast_add_fusion, f32[2,1024]{1,0:T(2,128)S(1)} %get-tuple-element.30, f32[2,1024]{1,0:T(2,128)S(1)} %get-tuple-element.31, f32[2,1024]{1,0:T(2,128)S(1)} %get-tuple-element.32, ...), kind=kLoop, calls=%fused_computation.60 | loop fusion | flops 14155776 | bytes 31498240 | tf_op jit(solution)/shard_map/jvp(vmap())/stack | solution.py:38
  191.5 12.2 %divide_bitcast_fusion = f32[1,2,1024,768]{3,2,1,0:T(8,128)} fusion(f32[2,1024,768]{2,1,0:T(8,128)S(1)} %broadcast_add_fusion, f32[2,2,768]{2,1,0:T(2,128)S(1)} %get-tuple-element.73, f32[2,1022,768]{2,1,0:T(8,128)} %get-tuple-element.75, f32[2,1022,768]{2,1,0:T(8,128)} %get-tuple-element.74, f32[2,2,768]{2,1,0:T(2,128)S(1)} %get-tuple-element.72, ...), kind=kLoop, calls=%fused_computation.58 | loop fusion | flops 22020096 | bytes 37797888 | tf_op jit(solution)/shard_map/jvp(vmap())/stack | solution.py:38
  203.8 12.4 %fusion.32 = f32[1,2,1024,768]{3,2,1,0:T(8,128)} fusion(f32[2,3,768]{2,1,0:T(4,128)S(1)} %get-tuple-element.77, f32[2,1021,768]{2,1,0:T(8,128)} %get-tuple-element.79, f32[2,1021,768]{2,1,0:T(8,128)} %get-tuple-element.78, f32[2,3,768]{2,1,0:T(4,128)S(1)} %get-tuple-element.76, f32[2,1024,768]{2,1,0:T(8,128)S(1)} %broadcast_add_fusion, ...), kind=kLoop, calls=%fused_computation.62 | loop fusion | flops 31457280 | bytes 50397184 | tf_op jit(solution)/shard_map/jvp(vmap())/stack | solution.py:38
  216.3 19.9 %pad_maximum_fusion = f32[4,2,1024,768]{3,2,1,0:T(8,128)} fusion(f32[1,2,1024,768]{3,2,1,0:T(8,128)} %fusion.32, f32[1,2,1024,768]{3,2,1,0:T(8,128)} %divide_bitcast_fusion, f32[1,2,1024,768]{3,2,1,0:T(8,128)} %get-tuple-element.67, f32[1,2,1024,768]{3,2,1,0:T(8,128)} %get-tuple-element.66), kind=kLoop, calls=%fused_computation.1 | loop fusion | flops 18874368 | bytes 50331648 | tf_op jit(solution)/shard_map/jvp(vmap())/stack | solution.py:38
  238.9 13.5 %fusion.142 = f32[1,4,2,1024]{3,0,2,1:T(1,128)S(1)} fusion(bf16[768,1,1,1]{0,1,2,3:T(2,128)(2,1)S(1)} %reshape.1243, f32[1,2,1024,768]{3,2,1,0:T(8,128)S(1)} %copy-done.8, f32[1,2,1024,768]{3,2,1,0:T(8,128)S(1)} %copy-done.7, f32[1,2,1024,768]{3,2,1,0:T(8,128)} %get-tuple-element.67, f32[1,2,1024,768]{3,2,1,0:T(8,128)S(1)} %copy-done.9), kind=kOutput, calls=%fused_computation.295 | convolution fusion | flops 94371840 | bytes 25200128 | tf_op jit(solution)/shard_map/jvp(vmap(agn,n->ga))/dot_general | solution.py:39
  252.8 10.2 %fusion.179 = (f32[2,1024]{1,0:T(2,128)S(1)}, f32[2,1024,1024]{2,1,0:T(8,128)S(1)}) fusion(f32[1,4,2,1024]{1,3,2,0:T(8,128)S(1)} %copy.111, pred[1024,1024]{1,0:T(8,128)(4,1)} %iota_compare_fusion, pred[2,1024]{1,0:T(4,128)(4,1)S(1)} %broadcast_compare_fusion.1, s32[2,1024]{1,0:T(2,128)S(1)} %convert_reduce_fusion.2), kind=kOutput, calls=%fused_computation.337 | convolution fusion | flops 111147008 | bytes 9488384 | tf_op jit(solution)/shard_map/jvp(vmap())/dot_general | solution.py:42
  263.1 3.3 copy-done.3
  268.1 12.2 %online-softmax = f32[2,1024,4]{2,1,0:T(8,128)} custom-call(f32[2,1024,1024]{2,1,0:T(8,128)} %copy-done.3, f32[2,1024,4]{2,1,0:T(8,128)} %bitcast.198), custom_call_target="tpu_custom_call" | custom-call | tf_op online-softmax
  282.7 114.6 %fusion.1 = f32[2,1024,1,4]{3,2,1,0:T(1,128)S(1)} fusion(f32[4,2,1024,768]{3,2,1,0:T(8,128)} %pad_maximum_fusion, f32[2,1024,768,1]{2,1,0,3:T(8,128)} %fusion.187), kind=kOutput, calls=%fused_computation.3 | convolution fusion | flops 75497472 | bytes 31490048 | tf_op jit(solution)/shard_map/transpose(jvp(vmap(ue,euh->uh)))/dot_general | solution.py:54
  399.3 7.1 fusion.5
  406.8 12.8 %convert_reduce_fusion = (f32[2,1024]{1,0:T(2,128)S(1)}, pred[2,1024,1024]{2,1,0:T(32,128)(4,1)S(1)}, f32[2,1024]{1,0:T(2,128)S(1)}, f32[2,1024,1024]{2,1,0:T(8,128)S(1)}) fusion(f32[2,1024,1024]{2,1,0:T(8,128)} %copy-done.3, f32[2,1024]{1,0:T(2,128)S(1)} %get-tuple-element.126, f32[2,1024]{1,0:T(2,128)S(1)} %multiply_divide_fusion, ...), kind=kOutput, calls=%fused_computation.8 | convolution fusion | flops 115396608 | bytes 19030016 | tf_op jit(solution)/shard_map/transpose(jvp(vmap()))/dot_general | solution.py:50
  419.6 5.6 fusion.155
  425.3 7.9 fusion.37
  433.3 10.7 %fusion.65 = f32[2,1024,4]{1,2,0:T(4,128)S(1)} fusion(f32[2,1024,4]{1,2,0:T(4,128)S(1)} %fusion.37, f32[2,1024,4]{1,2,0:T(4,128)S(1)} %copy-done.47, f32[2,1024,1024]{2,1,0:T(8,128)S(1)} %get-tuple-element.27, pred[2,1024,1024]{2,1,0:T(32,128)(4,1)S(1)} %get-tuple-element.29, f32[2,1024]{1,0:T(2,128)S(1)} %negate_divide_fusion, ...), kind=kOutput, calls=%fused_computation.116 | convolution fusion | flops 113262592 | bytes 11683840 | tf_op jit(solution)/shard_map/transpose(jvp(vmap()))/dot_general | solution.py:42
  444.1 3.5 bitcast_add_fusion
  447.6 7.6 broadcast_multiply_fusion.7
  455.2 6.3 copy-done
  462.4 7.2 split.124
  472.6 16.6 %broadcast_multiply_fusion.1 = (f32[2,1024,768]{2,1,0:T(8,128)S(1)}, f32[2,1024,768]{2,1,0:T(8,128)}, f32[2,1024,768]{2,1,0:T(8,128)}, f32[2,1024,768]{2,1,0:T(8...) fusion(f32[2,1024]{1,0:T(2,128)S(1)} %copy-done.29, ...), kind=kLoop, calls=%fused_computation.97 | loop fusion | flops 15728640 | bytes 62996480 | tf_op jit(solution)/shard_map/transpose(jvp(vmap()))/mul | solution.py:35
  490.0 7.2 split.114
  498.2 5.8 split.130
  513.3 35.5 %convert_reduce_fusion.1 = (f32[768]{0:T(1024)S(1)}, bf16[2,1024,768]{2,1,0:T(8,128)(2,1)S(1)}) fusion(f32[2,1024]{1,0:T(2,128)S(1)} %copy-done.25, f32[4,2,1024,768]{3,2,1,0:T(8,128)} %copy-done, f32[2,1,768]{2,1,0:T(1,128)S(1)} %split.131, f32[2,1023,768]{2,1,0:T(8,128)} %split.130, f32[2,1024]{1,0:T(2,128)S(1)} %get-tuple-element.32, ...), kind=kLoop, calls=%fused_computation.57 | loop fusion | flops 59768064 | bytes 103853056 | tf_op jit(solution)/shard_map/reduce_sum | solution.py:118
  548.9 20.0 %fusion.34 = f32[2,1024,5,768]{3,1,0,2:T(8,128)} fusion(bf16[5,768,768]{2,1,0:T(8,128)(2,1)} %all-gather.2.cloned.1.call-done, bf16[2,1024,768]{2,1,0:T(8,128)(2,1)S(1)} %get-tuple-element.17), kind=kOutput, calls=%fused_computation.64 | convolution fusion | flops 12079595520 | bytes 40501248 | tf_op jit(solution)/shard_map/rld,cd->rlc/dot_general | solution.py:125
  568.9 12.1 %fusion.8 = (f32[2,1024,768]{2,1,0:T(8,128)S(1)}, f32[2,1024,768]{2,1,0:T(8,128)}, f32[2,1024,768]{2,1,0:T(8,128)S(1)}, f32[2,1024,768]{2,1,0:T(8,128)S(1)}) fusion(f32[2,1024,5,768]{3,1,0,2:T(8,128)} %fusion.34, f32[2,1024]{1,0:T(2,128)S(1)} %copy-done.37, f32[2,1024]{1,0:T(2,128)S(1)} %copy-done.38, f32[2,1024]{1,0:T(2,128)S(1)} %copy-done.39, ...), kind=kLoop, calls=%fused_computation.17 | loop fusion | flops 6291456 | bytes 50364416 | tf_op jit(solution)/shard_map/mul | solution.py:132
  581.0 3.5 slice.382
  584.5 3.6 slice.379
  590.3 11.5 %fusion.61 = f32[256,768]{0,1:T(8,128)} fusion(f32[2,1024,5,768]{3,1,0,2:T(8,128)} %fusion.34, f32[2,2,768]{2,1,0:T(2,128)S(1)} %slice.380, f32[2,1022,768]{2,1,0:T(8,128)} %slice.379, f32[2,1,768]{2,1,0:T(1,128)S(1)} %slice.383, f32[2,1023,768]{2,1,0:T(8,128)S(1)} %copy-done.12, f32[2,1023,768]{2,1,0:T(8,128)S(1)} %bitcast.197, ...), kind=kOutput, calls=%fused_computation.114 | convolution fusion | flops 823132160 | bytes 32276480 | tf_op jit(solution)/shard_map/rlv,rld->vd/dot_general | solution.py:136
  601.9 18.5 %fusion.180 = f32[3840,768,1]{1,0,2:T(8,128)} fusion(bf16[2,1024,3840]{2,1,0:T(8,128)(2,1)} %fusion.56, bf16[2,1024,768]{2,1,0:T(8,128)(2,1)} %copy-done.15), kind=kOutput, calls=%fused_computation.338 | convolution fusion | flops 12079595520 | bytes 30670848 | tf_op jit(solution)/shard_map/rlc,rld->cd/dot_general | solution.py:119
  622.5 49.0 %psum.42 = f32[]{:T(128)} all-reduce(f32[]{:T(128)} %multiply_reduce_fusion.2), channel_id=1, replica_groups=mesh['fsdp'=8,'dp'=4] {'fsdp','dp'}, use_global_device_ids=true, to_apply=%region_10.11 | all-reduce | flops 1 | bytes 8 | tf_op jit(solution)/shard_map/psum | solution.py:114
  671.5 15.1 %fusion.66 = f32[768]{0:T(1024)S(1)} fusion(f32[4,2,1024,1]{2,0,1,3:T(4,128)S(1)} %bitcast.203, f32[1,2,1024,768]{3,2,1,0:T(8,128)} %fusion.32, f32[1,2,1024,768]{3,2,1,0:T(8,128)} %divide_bitcast_fusion, f32[1,2,1024,768]{3,2,1,0:T(8,128)} %get-tuple-element.67, f32[1,2,1024,768]{3,2,1,0:T(8,128)} %get-tuple-element.66), kind=kOutput, calls=%fused_computation.118 | convolution fusion | flops 94371840 | bytes 25201664 | tf_op jit(solution)/shard_map/transpose(jvp(vmap(agn,n->ga)))/dot_general | solution.py:39
  686.6 73.2 %fusion.3 = f32[2,1024,1,768]{3,2,1,0:T(1,128)} fusion(f32[2,1024,4,1]{2,3,1,0:T(1,128)S(1)} %bitcast.193, f32[4,2,1024,768]{3,2,1,0:T(8,128)} %pad_maximum_fusion), kind=kOutput, calls=%fused_computation.5 | convolution fusion | flops 75497472 | bytes 31490048 | tf_op jit(solution)/shard_map/jvp(vmap(ue,euh->uh))/dot_general | solution.py:54
  759.9 111.9 %reduce-scatter.5.cloned.1.call-done = f32[5,96,768]{2,1,0:T(8,128)} async-done(((f32[5,768,768]{2,1,0:T(8,128)}), f32[5,96,768]{2,1,0:T(8,128)}) %reduce-scatter.5.cloned.1.call-update) | async-done | bytes 1474576 | tf_op jit(solution)/shard_map/reduce_scatter | solution.py:141
  871.9 5.9 bitcast_multiply_fusion
  877.8 8.3 reshape.1227
  886.1 10.3 %reduce_sum.139 = f32[2,512,768]{2,1,0:T(8,128)S(1)} reduce(f32[2,512,2,768]{3,2,1,0:T(2,128)} %reshape.1227, f32[]{:T(128)} %constant.237.clone.1), dimensions={2}, to_apply=%region_6.7 | reduce | flops 786432 | bytes 9437188 | tf_op jit(solution)/shard_map/jvp(vmap())/reduce_sum | solution.py:61
  897.7 16.4 %all-reduce.28 = (f32[768]{0:T(1024)S(1)}, f32[768]{0:T(1024)S(1)}) all-reduce(f32[768]{0:T(1024)S(1)} %get-tuple-element.16, f32[768]{0:T(1024)S(1)} %fusion.66), channel_id=4, replica_groups=mesh['fsdp'=8,'dp'=4] {'fsdp'}, use_global_device_ids=true, to_apply=%region_23.24.clone | all-reduce | flops 1536 | bytes 12288
  914.3 9.6 %all-reduce.29 = (f32[96]{0:T(128)}, f32[96]{0:T(128)}) all-reduce(f32[96]{0:T(128)S(1)} %dynamic-slice.3, f32[96]{0:T(128)S(1)} %dynamic-slice.5), channel_id=1, replica_groups=mesh['fsdp'=8,'dp'=4] {'dp'}, use_global_device_ids=true, to_apply=%region_22.23 | all-reduce | flops 192 | bytes 1536 | tf_op jit(solution)/shard_map/psum | solution.py:138
  (242 shorter events, 62.9 us)
Async XLA Ops:
  7.2 137.0 %all-gather.2.cloned.1.call-start = ((), (), s32[]{:S(2)}) async-start(), calls=%async_computation.2 | async-start | bytes 6635520 | tf_op jit(solution)/shard_map/all_gather | solution.py:79
  7.9 752.0 %reduce-scatter.3.cloned.1.call-start = ((), (), s32[]{:S(2)}) async-start(), calls=%async_computation.3 | async-start | bytes 884736 | tf_op jit(solution)/shard_map/reduce_scatter | solution.py:140
  11.3 129.7 %copy-start.22 = (f32[2,1024]{1,0:T(2,128)}, f32[2,1024]{1,0:T(2,128)S(1)}, u32[]{:S(2)}) copy-start(f32[2,1024]{1,0:T(2,128)S(1)} %get-tuple-element.91) | copy-start | bytes 24580
  76.4 46.5 %copy-start.18 = (f32[2,1024]{1,0:T(2,128)}, f32[2,1024]{1,0:T(2,128)S(1)}, u32[]{:S(2)}) copy-start(f32[2,1024]{1,0:T(2,128)S(1)} %convert_element_type.140) | copy-start | bytes 24580
  84.3 10.0 %copy-start.30 = (bf16[256,96]{0,1:T(8,128)(2,1)S(1)}, bf16[256,96]{0,1:T(8,128)(2,1)}, u32[]{:S(2)}) copy-start(bf16[256,96]{0,1:T(8,128)(2,1)} %param.12) | copy-start | bytes 147460
  84.3 37.7 %copy-start.20 = (s32[2,1024]{1,0:T(2,128)S(1)}, s32[2,1024]{1,0:T(2,128)}, u32[]{:S(2)}) copy-start(s32[2,1024]{1,0:T(2,128)} %param.11) | copy-start | bytes 24580
  84.3 38.6 %copy-start.45 = (s32[2,1024]{1,0:T(2,128)S(1)}, s32[2,1024]{1,0:T(2,128)}, u32[]{:S(2)}) copy-start(s32[2,1024]{1,0:T(2,128)} %param.9) | copy-start | bytes 24580
  122.0 130.8 %copy-start.42 = (pred[2,1024]{1,0:T(4,128)(4,1)}, pred[2,1024]{1,0:T(4,128)(4,1)S(1)}, u32[]{:S(2)}) copy-start(pred[2,1024]{1,0:T(4,128)(4,1)S(1)} %broadcast_compare_fusion.1) | copy-start | bytes 6148
  122.9 55.5 %copy-start.24 = (f32[2,1024]{1,0:T(2,128)}, f32[2,1024]{1,0:T(2,128)S(1)}, u32[]{:S(2)}) copy-start(f32[2,1024]{1,0:T(2,128)S(1)} %get-tuple-element.30) | copy-start | bytes 24580
  124.6 79.2 %copy-start.26 = (f32[2,1024]{1,0:T(2,128)}, f32[2,1024]{1,0:T(2,128)S(1)}, u32[]{:S(2)}) copy-start(f32[2,1024]{1,0:T(2,128)S(1)} %get-tuple-element.45) | copy-start | bytes 24580
  124.6 79.2 %copy-start.28 = (f32[2,1024]{1,0:T(2,128)}, f32[2,1024]{1,0:T(2,128)S(1)}, u32[]{:S(2)}) copy-start(f32[2,1024]{1,0:T(2,128)S(1)} %get-tuple-element.46) | copy-start | bytes 24580
  178.4 13.1 %copy-start.1 = (f32[2,1023,768]{2,1,0:T(8,128)S(1)}, f32[2,1023,768]{2,1,0:T(8,128)}, u32[]{:S(2)}) copy-start(f32[2,1023,768]{2,1,0:T(8,128)} %get-tuple-element.70) | copy-start | bytes 18855940
  178.4 13.1 %copy-start.2 = (f32[2,1023,768]{2,1,0:T(8,128)S(1)}, f32[2,1023,768]{2,1,0:T(8,128)}, u32[]{:S(2)}) copy-start(f32[2,1023,768]{2,1,0:T(8,128)} %get-tuple-element.71) | copy-start | bytes 18855940
  178.4 25.4 %slice-start.2 = ((s8[6291456]{0:T(1024)(128)(4,1)}), s8[4194304]{0:T(1024)(128)(4,1)S(1)}, s32[]{:S(2)}) async-start(s8[6291456]{0:T(1024)(128)(4,1)} %bitcast.176), calls=%async_computation.8 | async-start | bytes 8388608
  178.4 25.4 %slice-start.4 = ((s8[6291456]{0:T(1024)(128)(4,1)}), s8[4194304]{0:T(1024)(128)(4,1)S(1)}, s32[]{:S(2)}) async-start(s8[6291456]{0:T(1024)(128)(4,1)} %bitcast.178), calls=%async_computation.10 | async-start | bytes 8388608
  191.5 12.3 %slice-start.3 = ((s8[6291456]{0:T(1024)(128)(4,1)}), s8[2097152]{0:T(1024)(128)(4,1)S(1)}, s32[]{:S(2)}) async-start(s8[6291456]{0:T(1024)(128)(4,1)} %bitcast.176), calls=%async_computation.9 | async-start | bytes 4194304
  191.5 12.3 %slice-start.5 = ((s8[6291456]{0:T(1024)(128)(4,1)}), s8[2097152]{0:T(1024)(128)(4,1)S(1)}, s32[]{:S(2)}) async-start(s8[6291456]{0:T(1024)(128)(4,1)} %bitcast.178), calls=%async_computation.11 | async-start | bytes 4194304
  216.3 19.9 %copy-start.7 = (f32[1,2,1024,768]{3,2,1,0:T(8,128)S(1)}, f32[1,2,1024,768]{3,2,1,0:T(8,128)}, u32[]{:S(2)}) copy-start(f32[1,2,1024,768]{3,2,1,0:T(8,128)} %divide_bitcast_fusion) | copy-start | bytes 18874372
  216.3 20.8 %copy-start.8 = (f32[1,2,1024,768]{3,2,1,0:T(8,128)S(1)}, f32[1,2,1024,768]{3,2,1,0:T(8,128)}, u32[]{:S(2)}) copy-start(f32[1,2,1024,768]{3,2,1,0:T(8,128)} %fusion.32) | copy-start | bytes 18874372
  216.3 22.7 %copy-start.9 = (f32[1,2,1024,768]{3,2,1,0:T(8,128)S(1)}, f32[1,2,1024,768]{3,2,1,0:T(8,128)}, u32[]{:S(2)}) copy-start(f32[1,2,1024,768]{3,2,1,0:T(8,128)} %get-tuple-element.66) | copy-start | bytes 18874372
  252.8 10.2 %copy-start.13 = (f32[1,4,2,1024]{1,3,2,0:T(8,128)}, f32[1,4,2,1024]{1,3,2,0:T(8,128)S(1)}, u32[]{:S(2)}) copy-start(f32[1,4,2,1024]{1,3,2,0:T(8,128)S(1)} %copy.111) | copy-start | bytes 98308
  280.3 119.0 %slice-start = ((s8[8388608]{0:T(1024)(128)(4,1)}), s8[4194304]{0:T(1024)(128)(4,1)S(1)}, s32[]{:S(2)}) async-start(s8[8388608]{0:T(1024)(128)(4,1)} %bitcast.174), calls=%async_computation.6 | async-start | bytes 8388608
  282.7 114.7 %copy-start.34 = (f32[2,1024]{1,0:T(2,128)S(1)}, f32[2,1024]{1,0:T(2,128)}, u32[]{:S(2)}) copy-start(f32[2,1024]{1,0:T(2,128)} %get-tuple-element.89) | copy-start | bytes 24580
  282.7 116.6 %slice-start.1 = ((s8[8388608]{0:T(1024)(128)(4,1)}), s8[4194304]{0:T(1024)(128)(4,1)S(1)}, s32[]{:S(2)}) async-start(s8[8388608]{0:T(1024)(128)(4,1)} %bitcast.174), calls=%async_computation.7 | async-start | bytes 8388608
  397.3 9.1 copy-start.16
  399.3 7.2 copy-start.10
  399.3 7.5 copy-start.14
  425.3 8.0 copy-start.47
  425.3 18.7 %slice-start.10 = ((s8[6291456]{0:T(1024)(128)(4,1)}), s8[4194304]{0:T(1024)(128)(4,1)S(1)}, s32[]{:S(2)}) async-start(s8[6291456]{0:T(1024)(128)(4,1)} %bitcast.190), calls=%async_computation.16 | async-start | bytes 8388608
  433.3 10.8 %slice-start.11 = ((s8[6291456]{0:T(1024)(128)(4,1)}), s8[2097152]{0:T(1024)(128)(4,1)S(1)}, s32[]{:S(2)}) async-start(s8[6291456]{0:T(1024)(128)(4,1)} %bitcast.190), calls=%async_computation.17 | async-start | bytes 4194304
  433.3 10.8 %copy-start.41 = (f32[768]{0:T(1024)S(1)}, f32[768]{0:T(1024)}, u32[]{:S(2)}) copy-start(f32[768]{0:T(1024)} %convert.3) | copy-start | bytes 9220
  447.6 14.0 %copy-start = (f32[4,2,1024,768]{3,2,1,0:T(8,128)}, f32[4,2,1024,768]{3,2,1,0:T(8,128)S(1)}, u32[]{:S(2)}) copy-start(f32[4,2,1024,768]{3,2,1,0:T(8,128)S(1)} %bitcast_add_fusion) | copy-start | bytes 75497472
  461.5 49.3 %copy-start.5 = (f32[2,1024,768]{2,1,0:T(8,128)}, f32[2,1024,768]{2,1,0:T(8,128)S(1)}, u32[]{:S(2)}) copy-start(f32[2,1024,768]{2,1,0:T(8,128)S(1)} %get-tuple-element.57) | copy-start | bytes 18874372
  462.4 7.2 copy-start.6
  489.2 24.1 %copy-start.4 = (f32[2,1024,768]{2,1,0:T(8,128)}, f32[2,1024,768]{2,1,0:T(8,128)S(1)}, u32[]{:S(2)}) copy-start(f32[2,1024,768]{2,1,0:T(8,128)S(1)} %get-tuple-element.51) | copy-start | bytes 18874372
  490.0 13.9 %slice-start.8 = ((s8[6291456]{0:T(1024)(128)(4,1)}), s8[4194304]{0:T(1024)(128)(4,1)S(1)}, s32[]{:S(2)}) async-start(s8[6291456]{0:T(1024)(128)(4,1)} %bitcast.185), calls=%async_computation.14 | async-start | bytes 8388608
  548.8 20.0 %copy-start.15 = (bf16[2,1024,768]{2,1,0:T(8,128)(2,1)}, bf16[2,1024,768]{2,1,0:T(8,128)(2,1)S(1)}, u32[]{:S(2)}) copy-start(bf16[2,1024,768]{2,1,0:T(8,128)(2,1)S(1)} %get-tuple-element.17) | copy-start | bytes 9437188
  548.8 20.0 %copy-start.37 = (f32[2,1024]{1,0:T(2,128)S(1)}, f32[2,1024]{1,0:T(2,128)}, u32[]{:S(2)}) copy-start(f32[2,1024]{1,0:T(2,128)} %get-tuple-element.18) | copy-start | bytes 24580
  548.8 20.0 %copy-start.38 = (f32[2,1024]{1,0:T(2,128)S(1)}, f32[2,1024]{1,0:T(2,128)}, u32[]{:S(2)}) copy-start(f32[2,1024]{1,0:T(2,128)} %get-tuple-element.108) | copy-start | bytes 24580
  548.8 20.0 %copy-start.39 = (f32[2,1024]{1,0:T(2,128)S(1)}, f32[2,1024]{1,0:T(2,128)}, u32[]{:S(2)}) copy-start(f32[2,1024]{1,0:T(2,128)} %get-tuple-element.110) | copy-start | bytes 24580
  548.8 20.0 %copy-start.40 = (f32[2,1024]{1,0:T(2,128)S(1)}, f32[2,1024]{1,0:T(2,128)}, u32[]{:S(2)}) copy-start(f32[2,1024]{1,0:T(2,128)} %get-tuple-element.112) | copy-start | bytes 24580
  581.0 7.2 slice-start.12
  601.9 270.0 %reduce-scatter.5.cloned.1.call-start = ((), (), s32[]{:S(2)}) async-start(), calls=%async_computation.4 | async-start | bytes 13271040 | tf_op jit(solution)/shard_map/reduce_scatter | solution.py:141
  620.5 51.0 %copy-start.36 = (f32[2,1024,4]{1,2,0:T(4,128)S(1)}, f32[2,1024,4]{1,2,0:T(4,128)}, u32[]{:S(2)}) copy-start(f32[2,1024,4]{1,2,0:T(4,128)} %copy-done.35) | copy-start | bytes 98308
  620.5 304.8 %all-reduce.34.cloned.1.call-start = ((), (), s32[]{:S(2)}) async-start(), calls=%async_computation.5 | async-start | bytes 3145728 | tf_op jit(solution)/shard_map/psum | solution.py:138
  671.5 15.1 %copy-start.11 = (f32[2,1024,4]{2,1,0:T(8,128)S(1)}, f32[2,1024,4]{2,1,0:T(8,128)}, u32[]{:S(2)}) copy-start(f32[2,1024,4]{2,1,0:T(8,128)} %copy-done.10) | copy-start | bytes 98308
  686.6 185.2 %copy-start.23 = (f32[2,1024]{1,0:T(2,128)S(1)}, f32[2,1024]{1,0:T(2,128)}, u32[]{:S(2)}) copy-start(f32[2,1024]{1,0:T(2,128)} %copy-done.22) | copy-start | bytes 24580
  886.1 37.9 %copy-start.32 = (f32[2,512]{1,0:T(2,128)S(1)}, f32[2,512]{1,0:T(2,128)}, u32[]{:S(2)}) copy-start(f32[2,512]{1,0:T(2,128)} %copy-done.31) | copy-start | bytes 12292
  (18 other events, 83.4 us)
Sparse Core Ops, SparseCore 0:
  10.2 98.9 all-gather.1
  602.0 68.7 reduce-scatter.2
  674.8 196.9 reduce-scatter.4
  874.1 41.9 all-reduce.33
where the time goes:
time: 943 us; the launch traced here: 937 us
  matrix products  334 us (35%)
  other arithmetic  190 us (20%)
  blocking collectives  161 us (17%)
  waiting for transfers between devices  113 us (12%)
  local copies, waits for them, and re-layouts  107 us (11%)
  between operations  20 us (2%)
  Pallas kernels  12.2 us (1%)
    dot_general x2, matrix products, latent_row(): jnp.einsum('ue,euh->uh', block_size_weight, block_average_values, precisi...  188 us
    reduce_scatter x1, waiting for transfers between devices, shards(): lax.psum_scatter(summed[1], 'fsdp', scatter_dimension=1, tiled=True)  112 us
    another operation x4, other arithmetic, latent_row(): block_average_values = jnp.stack(mean_list)  57.6 us
    psum x1, blocking collectives, shards(): entropy_total = lax.psum(entropy_here, ('fsdp', 'dp'))  49 us
    psum x1, blocking collectives, shards(): total_count = lax.psum(count_here, ('fsdp', 'dp'))  43.4 us
    reduce_sum x1, other arithmetic, shards(): bias_grad = jnp.sum(hidden_low.astype(jnp.float32), axis=(0, 1))  35.5 us
    split x18, local copies, waits for them, and re-layouts, latent_row(): jnp.roll(hidden, -offset, axis=0) * weight_here[:, None]  35.1 us
    unnamed x2, blocking collectives  33.1 us
  transfers between devices with their start and end apart: 4, of which 1 were waited for; matrix products, arithmetic and copies ran while one was open for 19% of the time, Pallas kernels for 0%

commit v1 on v0

v1 whole, which is shorter than its diff:
```python
import functools
import jax
import jax.numpy as jnp
from jax import lax
from jax.experimental import pallas as pl
from jax.experimental.pallas import tpu as pltpu
from jax.sharding import PartitionSpec as P

TAPS = 5
SIZES = 4
NEG = -1000000000.0
F32 = jnp.float32
BF16 = jnp.bfloat16
TILE = 256
EDGE = 16


def split2(x):
    high = x.astype(BF16).astype(F32)
    return high, x - high


def shift(x, offset):
    length = x.shape[1]
    return x if offset == 0 else pltpu.roll(x, (-offset) % length, 1)


def group_pair(x, step, lane_bit):
    size = x.shape[0]
    down = pltpu.roll(x, (size - step) % size, 0)
    up = pltpu.roll(x, step, 0)
    return jnp.where(lane_bit, up, down)


def group_all(x, op, bits):
    x = op(x, group_pair(x, 1, bits[0]))
    return op(x, group_pair(x, 2, bits[1]))


def spread(rows_list, length):
    return jnp.concatenate([jnp.broadcast_to(x, (SIZES, length)) for x in rows_list], axis=0)


def lane_rows(ref, at, r, length):
    return ref[at : at + 1, r * length : (r + 1) * length]


DELTA_EVEN = {-3: -2, -2: -1, -1: -1, 0: 0, 1: 0, 2: 1, 3: 1}
DELTA_ODD = {-3: -1, -2: -1, -1: 0, 0: 0, 1: 1, 2: 1, 3: 2}
OFFSETS = [o for o in range(1 - SIZES, SIZES) if o != 0]


def row_masks(rows, length, len_ref, ids_ref, mask_ref, taps_s):
    place1 = lax.broadcasted_iota(jnp.int32, (1, length), 1)
    seg_list, real_list = [], []
    for r in range(rows):
        end = len_ref[r, 0]
        segment = jnp.where(place1 >= end, 1.0, 0.0)
        for d in range(1, len_ref.shape[1]):
            end = end + len_ref[r, d]
            segment = segment + jnp.where(place1 >= end, 1.0, 0.0)
        seg_list.append(segment)
        real_list.append(mask_ref[r : r + 1, :].astype(F32))
        ids = ids_ref[r : r + 1, :].astype(F32)
        known = jnp.where(real_list[r] > 0.5, ids, -1.0)
        for k in range(TAPS):
            o = k - TAPS // 2
            inside = (place1 + o >= 0) & (place1 + o < length)
            keep = inside & (shift(segment, o) == segment)
            taps_s[k : k + 1, r * length : (r + 1) * length] = jnp.where(
                keep, shift(known, o), -1.0
            ).astype(jnp.int32)
    return seg_list, real_list


def fill_onehot(count, vocab, taps_s, onehot_s):
    symbol = lax.broadcasted_iota(jnp.int32, (vocab, TILE), 0)

    def step(t, carry):
        lanes = pl.ds(pl.multiple_of(t * TILE, TILE), TILE)
        for k in range(TAPS):
            here = taps_s[k : k + 1, lanes]
            onehot_s[k * vocab : (k + 1) * vocab, lanes] = jnp.where(symbol == here, 1.0, 0.0).astype(BF16)
        return carry

    lax.fori_loop(0, count, step, 0)


def members_of(rows, length, seg_list, real_list):
    shape = (rows * SIZES, length)
    place = lax.broadcasted_iota(jnp.int32, shape, 1)
    sub = lax.broadcasted_iota(jnp.int32, shape, 0)
    size = (sub & (SIZES - 1)) + 1
    third = jnp.floor((place.astype(F32) + 0.5) * (1.0 / 3.0)).astype(jnp.int32)
    within = jnp.where(
        size == 1, 0, jnp.where(size == 2, place & 1, jnp.where(size == 3, place - 3 * third, place & 3))
    )
    seg = spread(seg_list, length)
    real = spread(real_list, length)
    same = {}
    for o in range(1, SIZES):
        ahead = (within + o < size) & (place + o < length) & (shift(seg, o) == seg)
        behind = (within - o >= 0) & (shift(seg, -o) == seg)
        same[o] = jnp.where(ahead, 1.0, 0.0)
        same[-o] = jnp.where(behind, 1.0, 0.0)
    member = {o: same[o] * shift(real, o) for o in OFFSETS}
    members = real
    for o in OFFSETS:
        members = members + member[o]
    even = (place & 1) == 0
    pair = jnp.where(even | (shift(seg, -1) == seg), real, 0.0)
    partner = jnp.where(even, shift(pair, 1), shift(pair, -1))
    return dict(
        bits=((sub & 1) == 1, (sub & 2) == 2),
        first=size == 1,
        even=even,
        real=real,
        same=same,
        member=member,
        inverse=1.0 / jnp.maximum(members, 1.0),
        pair_weight=pair / jnp.maximum(pair + partner, 1.0),
    )


def block_scores(rows, length, m, q_s):
    q = spread([lane_rows(q_s, 0, r, length) for r in range(rows)], length)
    total = q * m["real"]
    for o in OFFSETS:
        total = total + m["member"][o] * shift(q, o)
    return total * m["inverse"]


def calibrate_row(r, length, scores, seg, real, similar_s, probs_s, between):
    s = scores[r * SIZES : (r + 1) * SIZES]
    a, rest = split2(s)
    b, c = split2(rest)
    key_seg = jnp.where(real > 0.5, seg, -1.0)
    zero = jnp.zeros((128 - 6 * SIZES - 1, length), F32)
    left = jnp.concatenate([a, a, b, b, a, c, key_seg, zero], axis=0).T
    right = jnp.concatenate([a, b, a, b, c, a, jnp.zeros_like(key_seg), zero], axis=0).astype(BF16)
    key_column = left[:, 6 * SIZES : 6 * SIZES + 1]
    left = left.astype(BF16)
    x = jnp.concatenate(
        [jnp.ones((1, length), F32), s, s[0:1] * s, s[1:2] * s[1:], s[2:3] * s[2:], s[3:4] * s[3:]]
        + [jnp.zeros((1, length), F32)],
        axis=0,
    )
    x_high, x_low = split2(x)
    features = jnp.concatenate([x_high, x_low], axis=0).astype(BF16)
    outs = []
    for t in range(length // TILE):
        lanes = slice(t * TILE, (t + 1) * TILE)
        query_seg = seg[:, lanes]
        top = None
        for j in range(length // 128):
            keys = slice(j * 128, (j + 1) * 128)
            sim = jnp.dot(left[keys], right[:, lanes], preferred_element_type=F32)
            allowed = key_column[keys] == query_seg
            if j * 128 // TILE == t:
                key_place = lax.broadcasted_iota(jnp.int32, (128, TILE), 0) + j * 128
                query_place = lax.broadcasted_iota(jnp.int32, (128, TILE), 1) + t * TILE
                allowed = allowed | (key_place == query_place)
            sim = jnp.where(allowed, sim, NEG)
            similar_s[keys, :] = sim
            here = jnp.max(sim, axis=0, keepdims=True)
            top = here if top is None else jnp.maximum(top, here)
        for j in range(length // 128):
            keys = slice(j * 128, (j + 1) * 128)
            probs_s[r, keys, lanes] = jnp.exp(similar_s[keys, :] - top).astype(BF16)
        outs.append(jnp.dot(features, probs_s[r, :, lanes], preferred_element_type=F32))
        between(r, t)
    moments = jnp.concatenate(outs, axis=1)
    moments = moments[0:16] + moments[16:32]
    norm = 1.0 / moments[0:1]
    return moments * norm, norm


def size_softmax(cal, bits):
    top = group_all(cal, jnp.maximum, bits)
    log_weight = (cal - top) - jnp.log(group_all(jnp.exp(cal - top), jnp.add, bits))
    weight = jnp.exp(log_weight)
    entropy = -group_all(weight * log_weight, jnp.add, bits)
    return weight, log_weight, entropy


def band_products(rows, length, cot_s, hidden_s, band_s, window):
    kl = lax.broadcasted_iota(jnp.int32, (window, TILE), 0)
    jl = lax.broadcasted_iota(jnp.int32, (window, TILE), 1) // 2 + EDGE
    diagonal = kl - jl
    for r in range(rows):
        for t in range(length // TILE):
            lanes = slice(r * length + t * TILE, r * length + (t + 1) * TILE)
            first = t * TILE // 2
            prod = jnp.dot(
                cot_s[r, first : first + window, :], hidden_s[:, lanes], preferred_element_type=F32
            )
            for d in range(-2, 3):
                band_s[d + 2 : d + 3, lanes] = jnp.sum(jnp.where(diagonal == d, prod, 0.0), axis=0, keepdims=True)
    return diagonal


def calibrate_back(r, length, scores, cal_grad, inner, moments, norm, probs_s):
    part = slice(r * SIZES, (r + 1) * SIZES)
    s, g, ri = scores[part], cal_grad[part], inner[r * SIZES : r * SIZES + 1]
    at = {}
    n = 1 + SIZES
    for a in range(SIZES):
        for b in range(a, SIZES):
            at[a, b] = at[b, a] = n
            n += 1
    query = []
    for a in range(SIZES):
        total = -moments[1 + a : 2 + a] * ri
        for b in range(SIZES):
            total = total + moments[at[a, b] : at[a, b] + 1] * g[b : b + 1]
        query.append(total)
    y = jnp.concatenate([g - s * ri] + [s[a : a + 1] * g for a in range(SIZES)], axis=0) * norm
    y = jnp.concatenate([y, jnp.zeros((4, length), F32)], axis=0)
    y_high, y_low = split2(y)
    features = jnp.concatenate([y_high, y_low], axis=0).astype(BF16)
    outs = []
    for t in range(length // TILE):
        keys = slice(t * TILE, (t + 1) * TILE)
        outs.append(
            lax.dot_general(features, probs_s[r, keys, :], (((1,), (1,)), ((), ())), preferred_element_type=F32)
        )
    back = jnp.concatenate(outs, axis=1)
    back = back[0:24] + back[24:48]
    key = []
    for a in range(SIZES):
        total = back[a : a + 1]
        for b in range(SIZES):
            n = SIZES + a * SIZES + b
            total = total + s[b : b + 1] * back[n : n + 1]
        key.append(total + query[a])
    return jnp.concatenate(key, axis=0)


def middle(dims, m, scores, seg_list, real_list, scale, scorer, refs, between):
    rows, length, width, vocab = dims
    half = length // 2
    tiles = length // TILE
    window = TILE // 2 + 2 * EDGE
    hidden_s, cot_s, band_s, pooled_s, hgrad_s, probs_s, similar_s, blocks_ref, part_ref, late_hidden = refs
    bits, real, same, member, inverse, pair_weight = (
        m[n] for n in ("bits", "real", "same", "member", "inverse", "pair_weight")
    )
    kept = [
        calibrate_row(r, length, scores, seg_list[r], real_list[r], similar_s, probs_s, between) for r in range(rows)
    ]
    cal = jnp.concatenate([moments[1 : 1 + SIZES] for moments, norm in kept], axis=0)
    weight, log_weight, entropy = size_softmax(cal, bits)
    entropy_sum = jnp.sum(
        jnp.sum(jnp.where(m["first"], entropy * real, 0.0), axis=1, keepdims=True), axis=0, keepdims=True
    )
    part_ref[...] = jnp.zeros_like(part_ref)
    part_ref[1:2, :] = jnp.broadcast_to(entropy_sum, (1, width))
    for r in range(rows):
        pooled_s[r] = jnp.zeros_like(pooled_s[r])

    late_hidden()
    diagonal = band_products(rows, length, cot_s, hidden_s, band_s, window)
    even1 = (lax.broadcasted_iota(jnp.int32, (1, length), 1) & 1) == 0
    band = [[lane_rows(band_s, d + 2, r, length) for d in range(-2, 3)] for r in range(rows)]

    def product(o):
        return spread(
            [jnp.where(even1, band[r][DELTA_EVEN[o] + 2], band[r][DELTA_ODD[o] + 2]) for r in range(rows)], length
        )

    gathered = real * product(0)
    for o in OFFSETS:
        gathered = gathered + member[o] * shift(product(-o), o)
    weight_grad = pair_weight * inverse * gathered
    cal_grad = weight * (weight_grad - group_all(weight * weight_grad, jnp.add, bits))
    cal_grad = cal_grad - scale() * real * weight * (log_weight + entropy)
    inner = group_all(cal * cal_grad, jnp.add, bits)
    score_grad = jnp.concatenate(
        [calibrate_back(r, length, scores, cal_grad, inner, kept[r][0], kept[r][1], probs_s) for r in range(rows)],
        axis=0,
    )
    score_grad = score_grad * inverse
    q_grad = score_grad
    for o in OFFSETS:
        q_grad = q_grad + same[o] * shift(score_grad, o)
    q_grad = group_all(q_grad * real, jnp.add, bits)

    use = pair_weight * weight * inverse
    moved = {o: (use if o == 0 else same[o] * shift(use, o)) for o in range(1 - SIZES, SIZES)}
    mix = []
    for d in range(-2, 3):
        odd_sum = sum([moved[o] for o in moved if DELTA_ODD[o] == d], jnp.zeros_like(use))
        even_sum = sum([moved[o] for o in moved if DELTA_EVEN[o] == d], jnp.zeros_like(use))
        mix.append(group_all(jnp.where(m["even"], even_sum, odd_sum) * real, jnp.add, bits))

    scorer16 = jnp.concatenate([scorer, scorer, jnp.zeros((EDGE - 2, width), BF16)], axis=0)
    for r in range(rows):
        at = r * SIZES
        q_high, q_low = split2(q_grad[at : at + 1])
        for t in range(tiles):
            lanes = slice(t * TILE, (t + 1) * TILE)
            all_lanes = slice(r * length + t * TILE, r * length + (t + 1) * TILE)
            first = t * TILE // 2
            matrix = jnp.zeros((window, TILE), F32)
            for d in range(-2, 3):
                matrix = jnp.where(diagonal == d, mix[d + 2][at : at + 1, lanes], matrix)
            high, low = split2(matrix)
            matrix = jnp.concatenate(
                [high, low, q_high[:, lanes], q_low[:, lanes], jnp.zeros((EDGE - 2, TILE), F32)], axis=0
            ).astype(BF16)
            out = lax.dot_general(
                matrix, hidden_s[:, all_lanes], (((1,), (1,)), ((), ())), preferred_element_type=F32
            )
            pooled_s[r, first : first + window, :] += out[:window] + out[window : 2 * window]
            part_ref[0:1, :] += out[2 * window : 2 * window + 1] + out[2 * window + 1 : 2 * window + 2]
            here = cot_s[r, first : first + window, :]
            given = jnp.concatenate([here, here, scorer16], axis=0)
            hgrad_s[all_lanes, :] = lax.dot_general(
                matrix, given, (((0,), (0,)), ((), ())), preferred_element_type=F32
            ).astype(BF16)
        blocks_ref[r] = pooled_s[r, EDGE : EDGE + half, :].astype(BF16)


def fill_cotangent(rows, half, width, cot_ref, cot_s):
    cot_s[:, 0:EDGE, :] = jnp.zeros((rows, EDGE, width), BF16)
    cot_s[:, EDGE + half :, :] = jnp.zeros((rows, EDGE, width), BF16)
    for r in range(rows):
        cot_s[r, EDGE : EDGE + half, :] = cot_ref[r]


def fill_q(count, tq16, const, onehot_s, q_s):
    def step(t, carry):
        lanes = pl.ds(pl.multiple_of(t * TILE, TILE), TILE)
        got = jnp.dot(tq16, onehot_s[:, lanes], preferred_element_type=F32)
        q_s[0:1, lanes] = got[0:1] + got[1:2] + got[2:3] + const
        return carry

    lax.fori_loop(0, count, step, 0)


def fill_hidden(count, table, bias_column, onehot_s, hidden_s):
    def step(t, carry):
        lanes = pl.ds(pl.multiple_of(t * TILE, TILE), TILE)
        got = jnp.dot(table(), onehot_s[:, lanes], preferred_element_type=F32)
        hidden_s[:, lanes] = (got + bias_column).astype(BF16)
        return carry

    lax.fori_loop(0, count, step, 0)


def local_scratch(rows, length, width, vocab):
    half = length // 2
    return [
        pltpu.VMEM((8, rows * length), jnp.int32),
        pltpu.VMEM((TAPS * vocab, rows * length), BF16),
        pltpu.VMEM((width, rows * length), BF16),
        pltpu.VMEM((8, rows * length), F32),
        pltpu.VMEM((rows, length, length), BF16),
        pltpu.VMEM((length, TILE), F32),
        pltpu.VMEM((rows, half + 2 * EDGE, width), BF16),
        pltpu.VMEM((8, rows * length), F32),
        pltpu.VMEM((rows, half + 2 * EDGE, width), F32),
        pltpu.VMEM((rows * length, width), BF16),
    ]


def main_kernel(
    dims, len_ref, aux_ref, small_ref, ids_ref, mask_ref, table_ref, tq_ref, bias_ref, scorer_ref, cot_ref,
    blocks_ref, grad_ref, part_ref,
    taps_s, onehot_s, hidden_s, q_s, probs_s, similar_s, cot_s, band_s, pooled_s, hgrad_s,
):
    rows, length, width, vocab = dims
    count = rows * (length // TILE)
    seg_list, real_list = row_masks(rows, length, len_ref, ids_ref, mask_ref, taps_s)
    fill_cotangent(rows, length // 2, width, cot_ref, cot_s)
    fill_onehot(count, vocab, taps_s, onehot_s)
    m = members_of(rows, length, seg_list, real_list)
    fill_q(count, tq_ref[...], small_ref[1:2, 0:1], onehot_s, q_s)
    scores = block_scores(rows, length, m, q_s)

    def late_hidden():
        fill_hidden(count, lambda: table_ref[...], bias_ref[...], onehot_s, hidden_s)

    def scale():
        return aux_ref[0, 0] / small_ref[0:1, 0:1]

    refs = (hidden_s, cot_s, band_s, pooled_s, hgrad_s, probs_s, similar_s, blocks_ref, part_ref, late_hidden)
    middle(dims, m, scores, seg_list, real_list, scale, scorer_ref[...], refs, lambda r, t: None)

    def grad_step(k, carry):
        symbols = pl.ds(pl.multiple_of(k * vocab, vocab), vocab)
        for c in range(width // TILE):
            cols = slice(c * TILE, (c + 1) * TILE)
            grad_ref[symbols, cols] = jnp.dot(
                onehot_s[symbols, :], hgrad_s[:, cols], preferred_element_type=F32
            )
        return carry

    lax.fori_loop(0, TAPS, grad_step, 0)


def main_call(lengths, aux, small, ids, mask, table, tq, bias, scorer, cot):
    rows, length = ids.shape
    width = cot.shape[2]
    vocab = table.shape[1] // TAPS
    dims = (rows, length, width, vocab)
    vmem = pl.BlockSpec(memory_space=pltpu.VMEM)
    smem = pl.BlockSpec(memory_space=pltpu.SMEM)
    half = length // 2
    return pl.pallas_call(
        functools.partial(main_kernel, dims),
        out_shape=(
            jax.ShapeDtypeStruct((rows, half, width), BF16),
            jax.ShapeDtypeStruct((TAPS * vocab, width), F32),
            jax.ShapeDtypeStruct((8, width), F32),
        ),
        in_specs=[smem, smem] + [vmem] * 8,
        out_specs=(vmem, vmem, vmem),
        scratch_shapes=local_scratch(rows, length, width, vocab),
        compiler_params=pltpu.CompilerParams(vmem_limit_bytes=60 * 1024 * 1024),
        name="latent",
    )(lengths, aux, small, ids, mask, table, tq, bias, scorer, cot)


MESH = pl.DeviceIdType.MESH
ALL = slice(None)


def split3(x):
    a = x.astype(BF16).astype(F32)
    b = (x - a).astype(BF16).astype(F32)
    return a, b, x - a - b


def remote(src, dst, send, recv, device):
    return pltpu.make_async_remote_copy(
        src_ref=src, dst_ref=dst, send_sem=send, recv_sem=recv, device_id=device, device_id_type=MESH
    )


def device_at(c, x, y, z):
    return (z * 2 + y, x * 2 + c)


class Gather:
    def __init__(self, buf, me, send, recv):
        self.buf, self.me, self.send, self.recv = buf, me, send, recv
        self.rows = buf.shape[4] // 2
        self.copies = {}

    def part(self, c, x, y, z, half):
        return self.buf.at[c, x, y, z, pl.ds(half * self.rows, self.rows)]

    def go(self, n, ref, device):
        copy = remote(ref, ref, self.send.at[n], self.recv.at[n], device)
        copy.start()
        self.copies[n] = copy

    def along_z(self):
        c, x, y, z = self.me
        for half in range(2):
            for i in range(1, 4):
                self.go(half * 3 + i - 1, self.part(c, x, y, z, half), device_at(c, x, y, lax.rem(z + i, 4)))

    def across(self, half, step):
        c, x, y, z = self.me
        if step == 0:
            for i in range(3):
                self.copies[half * 3 + i].wait_recv()
            mine = got = self.part(c, x, y, ALL, half)
        elif step == 1:
            self.copies[6 + half].wait_recv()
            mine = self.part(c, ALL, y, ALL, half) if half == 0 else self.part(c, x, ALL, ALL, half)
            got = self.part(c, 1 - x, y, ALL, half) if half == 0 else self.part(c, x, 1 - y, ALL, half)
        else:
            self.copies[8 + half].wait_recv()
            got = self.part(c, ALL, 1 - y, ALL, half) if half == 0 else self.part(c, 1 - x, ALL, ALL, half)
        if step < 2:
            over_x = (half == 0) == (step == 0)
            to = device_at(c, 1 - x, y, z) if over_x else device_at(c, x, 1 - y, z)
            self.go(6 + 2 * step + half, mine, to)
        self.go(10 + 2 * step + half, got, device_at(1 - c, x, y, z))

    def steps(self):
        return [functools.partial(self.across, half, step) for step in range(3) for half in range(2)]

    def finish(self):
        for n in range(10, 16):
            self.copies[n].wait_recv()
        for copy in self.copies.values():
            copy.wait_send()


def place_of(slot, taps, per_tap):
    slot = jnp.minimum(slot, taps * per_tap - 1)
    tap = slot // per_tap
    return tap, slot - tap * per_tap


def static_place(tap, column, per_tap):
    slot = tap * per_tap + column
    return slot // 16, slot // 8 % 2, slot // 4 % 2, slot % 4


def step_kernel(
    dims,
    len_ref, aux_ref, ids_ref, mask_ref, emb_ref, conv_ref, bias_ref, scorer_ref, cot_ref,
    blocks_ref, loss_ref, embg_ref, convg_ref, biasg_ref, scoreg_ref,
    taps_s, onehot_s, hidden_s, q_s, probs_s, similar_s, cot_s, band_s, pooled_s, hgrad_s,
    blocks_s, part_s, conv_s, emb_s, convg_s,
    small_s, smalls_s, wcol_s, emball_s, tq_s, tqs_s, count_s, table_s,
    give_s, take_s, own_s, pass_s, came_s, zgive_s, zown_s, zcame_s, final_s, sums_s, sumr_s,
    local_sem, start_send, start_recv, half_sem, gather_send, gather_recv,
    core_send, core_recv, quad_send, quad_recv, line_send, line_recv, sum_send, sum_recv,
):
    rows, length, width, vocab, size, fs = dims
    half = length // 2
    count = rows * (length // TILE)
    per_tap = width // 128
    f, d = lax.axis_index("fsdp"), lax.axis_index("dp")
    z, y = f // 2, lax.rem(f, 2)
    x, c = d // 2, lax.rem(d, 2)
    me = (c, x, y, z)
    core = device_at(1 - c, x, y, z)

    barrier = pltpu.get_barrier_semaphore()
    peers = [(lax.rem(f + i, fs), d) for i in range(1, fs)]
    others = [core, device_at(c, 1 - x, y, z), device_at(c, 1 - x, 1 - y, z)]
    for peer in peers + others:
        pl.semaphore_signal(barrier, inc=1, device_id=peer, device_id_type=MESH)

    mid = vocab // 2
    my_half = pl.ds(pl.multiple_of(c * mid, mid), mid)
    my_tap, my_column = place_of(((c * 2 + x) * 2 + y) * 4 + z, TAPS, per_tap)
    local = [
        pltpu.make_async_copy(conv_ref, conv_s, local_sem.at[0]),
        pltpu.make_async_copy(emb_ref, emb_s, local_sem.at[1]),
        pltpu.make_async_copy(
            conv_ref.at[my_tap, :, pl.ds(pl.multiple_of(my_column * 128, 128), 128)], wcol_s.at[f], local_sem.at[2]
        ),
        pltpu.make_async_copy(emb_ref.at[my_half], emball_s.at[f, my_half], local_sem.at[3]),
    ]
    for r in range(rows):
        local.append(pltpu.make_async_copy(cot_ref.at[r], cot_s.at[r, pl.ds(EDGE, half)], local_sem.at[4 + r]))
    for copy in local:
        copy.start()
    real_here = jnp.sum(jnp.sum(mask_ref[...].astype(F32), axis=1, keepdims=True), axis=0, keepdims=True)
    small_s[...] = jnp.zeros_like(small_s)
    small_s[0:1, 0:size] = bias_ref[...].astype(F32)
    small_s[1:2, 0:size] = scorer_ref[...].astype(F32)
    small_s[2:3, :] = jnp.broadcast_to(real_here, (1, 128))
    smalls_s[f] = small_s[...]
    seg_list, real_list = row_masks(rows, length, len_ref, ids_ref, mask_ref, taps_s)

    pl.semaphore_wait(barrier, fs - 1 + 3)
    starts = []
    for i, peer in enumerate(peers):
        starts.append(remote(small_s, smalls_s.at[f], start_send.at[0, i], start_recv.at[0, i], peer))
        starts[-1].start()
    for i, peer in enumerate(peers):
        tap, column = place_of(((c * 2 + x) * 2 + lax.rem(peer[0], 2)) * 4 + peer[0] // 2, TAPS, per_tap)
        starts.append(
            remote(emb_ref.at[my_half], emball_s.at[f, my_half], start_send.at[1, i], start_recv.at[1, i], peer)
        )
        starts[-1].start()
        starts.append(
            remote(
                conv_ref.at[tap, :, pl.ds(pl.multiple_of(column * 128, 128), 128)],
                wcol_s.at[f],
                start_send.at[2, i],
                start_recv.at[2, i],
                peer,
            )
        )
        starts[-1].start()

    fill_onehot(count, vocab, taps_s, onehot_s)
    cot_s[:, 0:EDGE, :] = jnp.zeros((rows, EDGE, width), BF16)
    cot_s[:, EDGE + half :, :] = jnp.zeros((rows, EDGE, width), BF16)

    for i in range(fs - 1):
        starts[i].wait_recv()
    line = jnp.zeros((16, width), F32)
    real_sum = jnp.zeros((1, 1), F32)
    lane = lax.broadcasted_iota(jnp.int32, (128, width), 0)
    at = lax.broadcasted_iota(jnp.int32, (128, width), 1)
    for g in range(fs):
        pick = jnp.where((at == lane + g * size) & (lane < size), 1.0, 0.0).astype(BF16)
        both = jnp.concatenate([smalls_s[g], jnp.zeros((8, 128), F32)], axis=0)
        keep = lax.broadcasted_iota(jnp.int32, (16, 128), 0) < 2
        line = line + jnp.dot(jnp.where(keep, both, 0.0).astype(BF16), pick, preferred_element_type=F32)
        real_sum = real_sum + smalls_s[g][2:3, 0:1]
    count_s[0] = jnp.broadcast_to(real_sum, (8, 128))
    count_x = remote(
        count_s.at[0], count_s.at[1], half_sem.at[0], half_sem.at[1], device_at(c, 1 - x, y, z)
    )
    count_x.start()
    line16 = line.astype(BF16)
    bias_column = jnp.concatenate([line, jnp.zeros((112, width), F32)], axis=0).T[:, 0:1]
    const = jnp.sum(line[0:1] * line[1:2], axis=1, keepdims=True)
    scorer = line16[1:2]
    local[0].wait()
    local[1].wait()
    across = (((1,), (1,)), ((), ()))
    u = jnp.concatenate(
        [
            lax.dot_general(line16, conv_s[k], across, preferred_element_type=F32)[1:2]
            for k in range(TAPS)
        ],
        axis=0,
    )
    u = jnp.concatenate(list(split3(u)) + [jnp.zeros((1, size), F32)], axis=0).astype(BF16)
    tq = lax.dot_general(u, emb_s[...], across, preferred_element_type=F32)
    tq_s[...] = jnp.zeros_like(tq_s)
    tq_s[0:TAPS, :] = tq[0:TAPS] + tq[TAPS : 2 * TAPS] + tq[2 * TAPS : 3 * TAPS]
    tqs_s[f] = tq_s[...]
    tq_copies = []
    for i, peer in enumerate(peers):
        copy = remote(tq_s, tqs_s.at[f], start_send.at[3, i], start_recv.at[3, i], peer)
        copy.start()
        tq_copies.append(copy)

    for copy in local[2:4]:
        copy.wait()
    for i in range(fs - 1):
        starts[fs - 1 + 2 * i].wait_recv()
    emb_core = remote(
        emball_s.at[:, my_half], emball_s.at[:, my_half], half_sem.at[2], half_sem.at[3], core
    )
    emb_core.start()
    for i in range(fs - 1):
        starts[fs + 2 * i].wait_recv()
    emb_core.wait_recv()
    block = None
    for g in range(fs):
        term = lax.dot_general(wcol_s[g], emball_s[g], (((0,), (1,)), ((), ())), preferred_element_type=F32)
        block = term if block is None else block + term
    table_s[c, x, y, z] = block.astype(BF16)
    tables = Gather(table_s, me, gather_send.at[0], gather_recv.at[0])
    tables.along_z()

    count_x.wait_recv()
    count_s[2] = count_s[0] + count_s[1]
    count_c = remote(count_s.at[2], count_s.at[3], half_sem.at[4], half_sem.at[5], core)
    count_c.start()

    m = members_of(rows, length, seg_list, real_list)
    for copy in tq_copies:
        copy.wait_recv()
    tq = tqs_s[0]
    for g in range(1, fs):
        tq = tq + tqs_s[g]
    tq16 = jnp.concatenate(
        [
            jnp.concatenate(list(split3(tq[k : k + 1])) + [jnp.zeros((13, vocab), F32)], axis=0)
            for k in range(TAPS)
        ],
        axis=1,
    ).astype(BF16)
    fill_q(count, tq16, const, onehot_s, q_s)
    scores = block_scores(rows, length, m, q_s)

    steps = tables.steps()

    def between(r, t):
        if steps and (r, t) != (0, 0):
            steps.pop(0)()

    def whole(k):
        return jnp.concatenate(
            [table_s[static_place(k, j, per_tap)] for j in range(per_tap)], axis=0
        )

    def late_hidden():
        while steps:
            steps.pop(0)()
        tables.finish()
        fill_hidden(
            count, lambda: jnp.concatenate([whole(k) for k in range(TAPS)], axis=1), bias_column, onehot_s, hidden_s
        )
        for copy in local[4:]:
            copy.wait()
        count_c.wait_recv()

    def scale():
        return aux_ref[0, 0] / (count_s[2][0:1, 0:1] + count_s[3][0:1, 0:1])

    refs = (hidden_s, cot_s, band_s, pooled_s, hgrad_s, probs_s, similar_s, blocks_s, part_s, late_hidden)
    middle(dims[:4], m, scores, seg_list, real_list, scale, scorer, refs, between)
    blocks_out = pltpu.make_async_copy(blocks_s, blocks_ref, local_sem.at[0])
    blocks_out.start()

    sums_s[0] = part_s[...]
    sum_copies = [remote(sums_s.at[0], sumr_s.at[0], sum_send.at[0], sum_recv.at[0], core)]
    sum_copies[0].start()

    def product(slot):
        tap, column = place_of(jnp.minimum(slot, TAPS * per_tap - 2), TAPS, per_tap)
        symbols = pl.ds(pl.multiple_of(tap * vocab, vocab), vocab)
        lanes = pl.ds(pl.multiple_of(column * 128, 256), 256)
        return jnp.dot(onehot_s[symbols, :], hgrad_s[:, lanes], preferred_element_type=F32)

    def core_copy(p):
        return remote(give_s.at[p], take_s.at[p], core_send.at[p], core_recv.at[p], core)

    def give(p, carry):
        give_s[p] = product((1 - c) * 16 + 2 * p)
        core_copy(p).start()
        return carry

    lax.fori_loop(0, 8, give, 0)

    sum_copies[0].wait_recv()
    sums_s[1] = sums_s[0] + sumr_s[0]
    quad = [device_at(c, lax.rem(x + q // 2, 2), lax.rem(y + q % 2, 2), z) for q in range(4)]
    for q in range(1, 4):
        sum_copies.append(remote(sums_s.at[1], sumr_s.at[q], sum_send.at[q], sum_recv.at[q], quad[q]))
        sum_copies[-1].start()

    def quad_copy(t):
        q = 3 - t // 2
        to = device_at(c, lax.rem(x + q // 2, 2), lax.rem(y + lax.rem(q, 2), 2), z)
        return remote(pass_s.at[t], came_s.at[t], quad_send.at[t], quad_recv.at[t], to)

    def forward(t, carry):
        q = 3 - t // 2
        p = lax.rem(x + q // 2, 2) * 4 + lax.rem(y + lax.rem(q, 2), 2) * 2 + lax.rem(t, 2)
        got = product(c * 16 + 2 * p)
        core_copy(p).wait_recv()
        pass_s[t] = (got + take_s[p]).astype(BF16)
        quad_copy(t).start()
        return carry

    lax.fori_loop(0, 6, forward, 0)
    for t in range(2):
        p = x * 4 + y * 2 + t
        got = product(c * 16 + 2 * p)
        core_copy(p).wait_recv()
        own_s[t] = got + take_s[p]

    for q in range(1, 4):
        sum_copies[q].wait_recv()
    sums_s[2] = (sums_s[1] + sumr_s[1]) + (sumr_s[2] + sumr_s[3])
    for i in range(1, 4):
        to = device_at(c, x, y, lax.rem(z + i, 4))
        sum_copies.append(remote(sums_s.at[2], sumr_s.at[3 + i], sum_send.at[3 + i], sum_recv.at[3 + i], to))
        sum_copies[-1].start()

    for t in range(2):
        for q in range(1, 4):
            quad_copy(6 - 2 * q + t).wait_recv()
        total = own_s[t]
        for q in range(1, 4):
            total = total + came_s[6 - 2 * q + t].astype(F32)
        for j in range(2):
            zown_s[2 * t + j] = total[:, j * 128 : (j + 1) * 128]
            zgive_s[2 * t + j] = total[:, j * 128 : (j + 1) * 128].astype(BF16)
    line_copies = []
    for i in range(1, 4):
        to = lax.rem(z + i, 4)
        copy = remote(
            zgive_s.at[to], zcame_s.at[i - 1], line_send.at[i - 1], line_recv.at[i - 1], device_at(c, x, y, to)
        )
        copy.start()
        line_copies.append(copy)
    total = zown_s[z]
    for i, copy in enumerate(line_copies):
        copy.wait_recv()
        total = total + zcame_s[i].astype(F32)
    final_s[c, x, y, z] = total.astype(BF16)
    grads = Gather(final_s, me, gather_send.at[1], gather_recv.at[1])
    grads.along_z()

    for i in range(4, 7):
        sum_copies[i].wait_recv()
    sums = (sums_s[2] + sumr_s[4]) + (sumr_s[5] + sumr_s[6])
    loss_ref[...] = sums[1:2, 0:1] / (count_s[2][0:1, 0:1] + count_s[3][0:1, 0:1])

    for step in grads.steps():
        step()
    grads.finish()
    emb_total = None
    out_copies = []
    for k in range(TAPS):
        grad = jnp.concatenate([final_s[static_place(k, j, per_tap)] for j in range(per_tap)], axis=1)
        convg_s[k] = lax.dot_general(emb_s[...], grad, (((0,), (0,)), ((), ())), preferred_element_type=F32)
        out_copies.append(pltpu.make_async_copy(convg_s.at[k], convg_ref.at[k], local_sem.at[1 + k]))
        out_copies[-1].start()
        term = lax.dot_general(grad, conv_s[k], across, preferred_element_type=F32)
        emb_total = term if emb_total is None else emb_total + term
        if k == TAPS // 2:
            bias_line = jnp.sum(grad.astype(F32), axis=0, keepdims=True)
    embg_ref[...] = emb_total
    pick = jnp.where((at == lane + f * size) & (lane < size), 1.0, 0.0).astype(BF16)
    lines = jnp.concatenate(
        list(split3(bias_line)) + list(split3(sums[0:1])) + [jnp.zeros((10, width), F32)], axis=0
    ).astype(BF16)
    mine = lax.dot_general(lines, pick, across, preferred_element_type=F32)
    biasg_ref[...] = (mine[0:1] + mine[1:2] + mine[2:3])[:, :size]
    scoreg_ref[...] = (mine[3:4] + mine[4:5] + mine[5:6])[:, :size]

    for copy in starts + tq_copies + sum_copies + line_copies + [count_x, count_c, emb_core]:
        copy.wait_send()
    for p in range(8):
        core_copy(p).wait_send()
    for t in range(6):
        quad_copy(t).wait_send()
    for copy in out_copies + [blocks_out]:
        copy.wait()


def step_shards(byte_ids, doc_lengths, pad_mask, embedding, conv_weight, conv_bias, scorer, cotangent, aux_weight):
    rows, length = byte_ids.shape
    vocab, size = embedding.shape
    width = conv_weight.shape[2]
    half = length // 2
    fs = width // size
    dims = (rows, length, width, vocab, size, fs)
    vmem = pl.BlockSpec(memory_space=pltpu.VMEM)
    smem = pl.BlockSpec(memory_space=pltpu.SMEM)
    hbm = pl.BlockSpec(memory_space=pl.ANY)
    dma = pltpu.SemaphoreType.DMA
    blocks, loss, emb_grad, conv_grad, bias_grad, score_grad = pl.pallas_call(
        functools.partial(step_kernel, dims),
        out_shape=(
            jax.ShapeDtypeStruct((rows, half, width), BF16),
            jax.ShapeDtypeStruct((1, 1), F32),
            jax.ShapeDtypeStruct((vocab, size), F32),
            jax.ShapeDtypeStruct((TAPS, size, width), F32),
            jax.ShapeDtypeStruct((1, size), F32),
            jax.ShapeDtypeStruct((1, size), F32),
        ),
        in_specs=[smem, smem, vmem, vmem, hbm, hbm, vmem, vmem, hbm],
        out_specs=(hbm, vmem, vmem, hbm, vmem, vmem),
        scratch_shapes=local_scratch(rows, length, width, vocab)
        + [
            pltpu.VMEM((rows, half, width), BF16),
            pltpu.VMEM((8, width), F32),
            pltpu.VMEM((TAPS, size, width), BF16),
            pltpu.VMEM((vocab, size), BF16),
            pltpu.VMEM((TAPS, size, width), F32),
            pltpu.VMEM((8, 128), F32),
            pltpu.VMEM((fs, 8, 128), F32),
            pltpu.VMEM((fs, size, 128), BF16),
            pltpu.VMEM((fs, vocab, size), BF16),
            pltpu.VMEM((8, vocab), F32),
            pltpu.VMEM((fs, 8, vocab), F32),
            pltpu.VMEM((4, 8, 128), F32),
            pltpu.VMEM((2, 2, 2, 4, 128, vocab), BF16),
            pltpu.VMEM((8, vocab, 256), F32),
            pltpu.VMEM((8, vocab, 256), F32),
            pltpu.VMEM((2, vocab, 256), F32),
            pltpu.VMEM((6, vocab, 256), BF16),
            pltpu.VMEM((6, vocab, 256), BF16),
            pltpu.VMEM((4, vocab, 128), BF16),
            pltpu.VMEM((4, vocab, 128), F32),
            pltpu.VMEM((3, vocab, 128), BF16),
            pltpu.VMEM((2, 2, 2, 4, vocab, 128), BF16),
            pltpu.VMEM((3, 8, width), F32),
            pltpu.VMEM((7, 8, width), F32),
            dma((4 + max(rows, 2),)),
            dma((4, fs - 1)),
            dma((4, fs - 1)),
            dma((6,)),
            dma((2, 16)),
            dma((2, 16)),
            dma((8,)),
            dma((8,)),
            dma((6,)),
            dma((6,)),
            dma((3,)),
            dma((3,)),
            dma((7,)),
            dma((7,)),
        ],
        compiler_params=pltpu.CompilerParams(
            collective_id=0, has_side_effects=True, vmem_limit_bytes=62 * 1024 * 1024
        ),
        name="step",
    )(
        doc_lengths,
        aux_weight.reshape(1, 1),
        byte_ids,
        pad_mask,
        embedding,
        conv_weight,
        conv_bias.reshape(1, size),
        scorer.reshape(1, size),
        cotangent,
    )
    return blocks, loss.reshape(()), emb_grad, conv_grad, bias_grad.reshape(size), score_grad.reshape(size)


def split3_rows(x):
    a = lax.reduce_precision(x, 8, 7)
    b = lax.reduce_precision(x - a, 8, 7)
    return jnp.concatenate([a, b, x - a - b], axis=0).astype(BF16)


def gathered_shards(byte_ids, doc_lengths, pad_mask, embedding, conv_weight, conv_bias, scorer, cotangent, aux_weight):
    emb = lax.all_gather(embedding, "fsdp", axis=1, tiled=True)
    conv = lax.all_gather(conv_weight, "fsdp", axis=1, tiled=True)
    bias = lax.all_gather(conv_bias, "fsdp", axis=0, tiled=True)
    score = lax.all_gather(scorer, "fsdp", axis=0, tiled=True)
    vocab, width = emb.shape
    count = lax.psum(jnp.sum(pad_mask.astype(F32)), ("fsdp", "dp"))
    table = jnp.einsum("kcd,vc->dkv", conv, emb, preferred_element_type=F32).reshape(width, TAPS * vocab)
    score32 = score.astype(F32)
    q_table = jnp.sum(table * score32[:, None], axis=0, keepdims=True)
    tq = jnp.concatenate([split3_rows(q_table), jnp.zeros((13, TAPS * vocab), BF16)], axis=0)
    bias32 = bias.astype(F32)
    small = jnp.stack([jnp.full((128,), count), jnp.full((128,), jnp.sum(bias32 * score32))])
    small = jnp.concatenate([small, jnp.zeros((6, 128), F32)], axis=0)
    blocks, grad, part = main_call(
        doc_lengths, aux_weight.reshape(1, 1), small, byte_ids, pad_mask, table.astype(BF16), tq, bias32[:, None], score[None, :], cotangent
    )
    grad = lax.psum(grad, ("fsdp", "dp")).reshape(TAPS, vocab, width)
    score_grad = lax.psum(part[0], ("fsdp", "dp"))
    loss = lax.psum(part[1, 0], ("fsdp", "dp")) / count
    size = embedding.shape[1]
    at = lax.axis_index("fsdp") * size
    bias_grad = lax.dynamic_slice_in_dim(jnp.sum(grad[TAPS // 2], axis=0), at, size, 0)
    score_grad = lax.dynamic_slice_in_dim(score_grad, at, size, 0)
    conv_grad = jnp.einsum("vc,kvd->kcd", embedding.astype(F32), grad, precision=lax.Precision.HIGHEST)
    emb_grad = jnp.einsum("kvd,kcd->vc", grad, conv_weight.astype(F32), precision=lax.Precision.HIGHEST)
    return blocks, loss, emb_grad, conv_grad, bias_grad, score_grad


def solution(mesh):
    small = mesh.shape["fsdp"] == 8 and mesh.shape["dp"] == 4
    return jax.shard_map(
        step_shards if small else gathered_shards,
        mesh=mesh,
        in_specs=(
            P(("fsdp", "dp"), None),
            P(("fsdp", "dp"), None),
            P(("fsdp", "dp"), None),
            P(None, "fsdp"),
            P(None, "fsdp", None),
            P("fsdp"),
            P("fsdp"),
            P(("fsdp", "dp"), None, None),
            P(),
        ),
        out_specs=(
            P(("fsdp", "dp"), None, None),
            P(),
            P(None, "fsdp"),
            P(None, "fsdp", None),
            P("fsdp"),
            P("fsdp"),
        ),
        check_vma=False,
    )
```

time: 943 us -> 113 us (0.12)
  matrix products: 334 us -> 0 us
  other arithmetic: 190 us -> 0 us
  blocking collectives: 161 us -> 0 us
  waiting for transfers between devices: 113 us -> 0 us
  local copies, waits for them, and re-layouts: 107 us -> 8.08 us
  Pallas kernels: 12.2 us -> 101 us
  between operations: 20 us -> 3.11 us
    dot_general x14 -> x0, matrix products: 334 us -> none  [the longest x2 188 us: latent_row(): jnp.einsum('ue,euh->uh', block_size_weight, block_average_values, precisi...]
    reduce_scatter x2 -> x0, waiting for transfers between devices: 112 us -> none  [the longest x1 112 us: shards(): lax.psum_scatter(summed[1], 'fsdp', scatter_dimension=1, tiled=True)]
    psum x3 -> x0, blocking collectives: 102 us -> none  [the longest x1 49 us: shards(): entropy_total = lax.psum(entropy_here, ('fsdp', 'dp'))]
    pallas_call x0 -> x1, Pallas kernels: none -> 101 us  [step_shards(): pl.pallas_call(functools.partial(step_kernel, dims), out_shape=(jax.Shape...]
    another operation x6 -> x0, other arithmetic: 59 us -> none  [the longest x4 57.6 us: latent_row(): block_average_values = jnp.stack(mean_list)]
    reduce_sum x9 -> x0, other arithmetic: 57.3 us -> none  [the longest x1 35.5 us: shards(): bias_grad = jnp.sum(hidden_low.astype(jnp.float32), axis=(0, 1))]
    mul x6 -> x0, other arithmetic: 48.5 us -> none  [the longest x2 24.2 us: latent_row(): jnp.roll(hidden, -offset, axis=0) * weight_here[:, None]]
    split x18 -> x0, local copies, waits for them, and re-layouts: 35.1 us -> none  [latent_row(): jnp.roll(hidden, -offset, axis=0) * weight_here[:, None]]
  transfers between devices with their start and end apart: 4 -> 0, of which waited for: 1 -> 0; matrix products, arithmetic and copies ran while one was open for 19% -> 0% of each run, Pallas kernels for 0% -> 0%
where the time goes in v1:
time: 113 us; the launch traced here: 112 us
  Pallas kernels  101 us (89%)
  local copies, waits for them, and re-layouts  8.08 us (7%)
  between operations  3.11 us (3%)
    pallas_call x1, Pallas kernels, step_shards(): pl.pallas_call(functools.partial(step_kernel, dims), out_shape=(jax.Shape...  101 us
    unnamed x12, local copies, waits for them, and re-layouts  8.08 us

profile of v1, /device:TPU:1, one launch (start us, length us, event | category | flops | bytes accessed | tf_op | source)
XLA Modules:
  0.0 112.3 jit_solution(15103375886197005390)
XLA Ops:
  1.3 1.5 %copy.15.emb_ref = bf16[256,96]{1,0:T(8,128)(2,1)} copy(bf16[256,96]{0,1:T(8,128)(2,1)} %param.12) | data formatting | bytes 98304 | tf_op args[3]
  2.8 101.1 %step.1 = (bf16[2,512,768]{2,1,0:T(8,128)(2,1)}, f32[1,1]{1,0:T(1,128)}, f32[256,96]{1,0:T(8,128)}, f32[5,96,768]{2,1,0:T(8,128)}, f32[1,96]{1,0:T(1,128)}, /*index=5*/f32[1,96]{1,0:T(1,128)}) custom-call(s32[2,8]{1,0:T(2,128)} %len_ref.1, f32[1,1]{1,0:T(1,128)} %bitcast.6.aux_ref, s32[2,1024]{1,0:T(2,128)} %ids_ref.1, s32[2,1024]{1,0:T(2,128)} %mask_ref.1, ...), custom_call_target="tpu_custom_call" | custom-call | tf_op jit(solution)/shard_map/step/pallas_call | solution.py:823
  103.9 1.6 %copy.16 = f32[256,96]{0,1:T(8,128)} copy(f32[256,96]{1,0:T(8,128)} %get-tuple-element.20) | data formatting | bytes 196608
  105.5 0.0 copy-start
  105.5 2.8 %copy.23 = bf16[2,512,768]{2,1,0:T(8,128)(2,1)} copy(bf16[2,512,768]{2,1,0:T(8,128)(2,1)} %get-tuple-element.30) | data formatting | bytes 3145728
  108.3 0.0 copy-start.2
  108.3 0.0 copy-start.1
  109.0 0.0 copy-done
  109.0 1.1 copy.25
  110.1 0.0 copy-done.2
  110.1 0.5 copy.26
  110.6 0.0 copy-done.1
  110.6 0.5 copy.27
Async XLA Ops:
  105.5 3.5 %copy-start = (f32[5,96,768]{2,1,0:T(8,128)S(1)}, f32[5,96,768]{2,1,0:T(8,128)}, u32[]{:S(2)}) copy-start(f32[5,96,768]{2,1,0:T(8,128)} %get-tuple-element.33) | copy-start | bytes 4423684
  108.3 1.8 %copy-start.2 = (f32[1,96]{1,0:T(1,128)S(1)}, f32[1,96]{1,0:T(1,128)}, u32[]{:S(2)}) copy-start(f32[1,96]{1,0:T(1,128)} %get-tuple-element.16) | copy-start | bytes 1156
  108.3 2.3 %copy-start.1 = (f32[1,96]{1,0:T(1,128)S(1)}, f32[1,96]{1,0:T(1,128)}, u32[]{:S(2)}) copy-start(f32[1,96]{1,0:T(1,128)} %get-tuple-element.17) | copy-start | bytes 1156

commit v2 on v1

--- a/solution.py
+++ b/solution.py
@@ -13,6 +13,8 @@
 BF16 = jnp.bfloat16
 TILE = 256
 EDGE = 16
+TABLE_CHUNKS = 2
+GRAD_CHUNKS = 2
 
 
 def split2(x):
@@ -241,7 +243,7 @@
     half = length // 2
     tiles = length // TILE
     window = TILE // 2 + 2 * EDGE
-    hidden_s, cot_s, band_s, pooled_s, hgrad_s, probs_s, similar_s, blocks_ref, part_ref, late_hidden = refs
+    hidden_s, cot_s, band_s, pooled_s, hgrad_s, probs_s, similar_s, blocks_ref, part_ref, matrix_s, late_hidden = refs
     bits, real, same, member, inverse, pair_weight = (
         m[n] for n in ("bits", "real", "same", "member", "inverse", "pair_weight")
     )
@@ -308,17 +310,28 @@
             matrix = jnp.concatenate(
                 [high, low, q_high[:, lanes], q_low[:, lanes], jnp.zeros((EDGE - 2, TILE), F32)], axis=0
             ).astype(BF16)
-            out = lax.dot_general(
-                matrix, hidden_s[:, all_lanes], (((1,), (1,)), ((), ())), preferred_element_type=F32
-            )
-            pooled_s[r, first : first + window, :] += out[:window] + out[window : 2 * window]
-            part_ref[0:1, :] += out[2 * window : 2 * window + 1] + out[2 * window + 1 : 2 * window + 2]
+            matrix_s[r * tiles + t] = matrix
             here = cot_s[r, first : first + window, :]
             given = jnp.concatenate([here, here, scorer16], axis=0)
             hgrad_s[all_lanes, :] = lax.dot_general(
                 matrix, given, (((0,), (0,)), ((), ())), preferred_element_type=F32
             ).astype(BF16)
-        blocks_ref[r] = pooled_s[r, EDGE : EDGE + half, :].astype(BF16)
+
+    def pool():
+        for r in range(rows):
+            for t in range(tiles):
+                first = t * TILE // 2
+                out = lax.dot_general(
+                    matrix_s[r * tiles + t],
+                    hidden_s[:, r * length + t * TILE : r * length + (t + 1) * TILE],
+                    (((1,), (1,)), ((), ())),
+                    preferred_element_type=F32,
+                )
+                pooled_s[r, first : first + window, :] += out[:window] + out[window : 2 * window]
+                part_ref[0:1, :] += out[2 * window : 2 * window + 1] + out[2 * window + 1 : 2 * window + 2]
+            blocks_ref[r] = pooled_s[r, EDGE : EDGE + half, :].astype(BF16)
+
+    return pool
 
 
 def fill_cotangent(rows, half, width, cot_ref, cot_s):
@@ -361,13 +374,14 @@
         pltpu.VMEM((8, rows * length), F32),
         pltpu.VMEM((rows, half + 2 * EDGE, width), F32),
         pltpu.VMEM((rows * length, width), BF16),
+        pltpu.VMEM((rows * (length // TILE), TILE + 5 * EDGE, TILE), BF16),
     ]
 
 
 def main_kernel(
     dims, len_ref, aux_ref, small_ref, ids_ref, mask_ref, table_ref, tq_ref, bias_ref, scorer_ref, cot_ref,
     blocks_ref, grad_ref, part_ref,
-    taps_s, onehot_s, hidden_s, q_s, probs_s, similar_s, cot_s, band_s, pooled_s, hgrad_s,
+    taps_s, onehot_s, hidden_s, q_s, probs_s, similar_s, cot_s, band_s, pooled_s, hgrad_s, matrix_s,
 ):
     rows, length, width, vocab = dims
     count = rows * (length // TILE)
@@ -384,8 +398,9 @@
     def scale():
         return aux_ref[0, 0] / small_ref[0:1, 0:1]
 
-    refs = (hidden_s, cot_s, band_s, pooled_s, hgrad_s, probs_s, similar_s, blocks_ref, part_ref, late_hidden)
-    middle(dims, m, scores, seg_list, real_list, scale, scorer_ref[...], refs, lambda r, t: None)
+    refs = (hidden_s, cot_s, band_s, pooled_s, hgrad_s, probs_s, similar_s, blocks_ref, part_ref, matrix_s, late_hidden)
+    pool = middle(dims, m, scores, seg_list, real_list, scale, scorer_ref[...], refs, lambda r, t: None)
+    pool()
 
     def grad_step(k, carry):
         symbols = pl.ds(pl.multiple_of(k * vocab, vocab), vocab)
@@ -443,50 +458,55 @@
 
 
 class Gather:
-    def __init__(self, buf, me, send, recv):
-        self.buf, self.me, self.send, self.recv = buf, me, send, recv
-        self.rows = buf.shape[4] // 2
+    def __init__(self, buf, me, send, recv, chunks):
+        self.buf, self.me, self.send, self.recv, self.chunks = buf, me, send, recv, chunks
+        self.rows = buf.shape[4] // chunks
         self.copies = {}
 
-    def part(self, c, x, y, z, half):
-        return self.buf.at[c, x, y, z, pl.ds(half * self.rows, self.rows)]
-
-    def go(self, n, ref, device):
-        copy = remote(ref, ref, self.send.at[n], self.recv.at[n], device)
+    def part(self, c, x, y, z, chunk, half=None):
+        if half is None:
+            return self.buf.at[c, x, y, z, pl.ds(chunk * self.rows, self.rows)]
+        return self.buf.at[c, x, y, z, pl.ds(chunk * self.rows + half * (self.rows // 2), self.rows // 2)]
+
+    def go(self, chunk, n, ref, device):
+        at = chunk * 11 + n
+        copy = remote(ref, ref, self.send.at[at], self.recv.at[at], device)
         copy.start()
-        self.copies[n] = copy
-
-    def along_z(self):
+        self.copies[chunk, n] = copy
+
+    def along_z(self, chunk):
         c, x, y, z = self.me
-        for half in range(2):
-            for i in range(1, 4):
-                self.go(half * 3 + i - 1, self.part(c, x, y, z, half), device_at(c, x, y, lax.rem(z + i, 4)))
-
-    def across(self, half, step):
+        for i in range(1, 4):
+            self.go(chunk, i - 1, self.part(c, x, y, z, chunk), device_at(c, x, y, lax.rem(z + i, 4)))
+
+    def across(self, chunk, step):
         c, x, y, z = self.me
+        copies = self.copies
+        core, over_x, over_y = device_at(1 - c, x, y, z), device_at(c, 1 - x, y, z), device_at(c, x, 1 - y, z)
         if step == 0:
-            for i in range(3):
-                self.copies[half * 3 + i].wait_recv()
-            mine = got = self.part(c, x, y, ALL, half)
+            for n in range(3):
+                copies[chunk, n].wait_recv()
+            mine = self.part(c, x, y, ALL, chunk)
+            self.go(chunk, 3, mine, over_x)
+            self.go(chunk, 4, mine, over_y)
+            self.go(chunk, 5, mine, core)
         elif step == 1:
-            self.copies[6 + half].wait_recv()
-            mine = self.part(c, ALL, y, ALL, half) if half == 0 else self.part(c, x, ALL, ALL, half)
-            got = self.part(c, 1 - x, y, ALL, half) if half == 0 else self.part(c, x, 1 - y, ALL, half)
+            copies[chunk, 3].wait_recv()
+            self.go(chunk, 6, self.part(c, 1 - x, y, ALL, chunk, 0), over_y)
+            self.go(chunk, 7, self.part(c, 1 - x, y, ALL, chunk), core)
+            copies[chunk, 4].wait_recv()
+            self.go(chunk, 8, self.part(c, x, 1 - y, ALL, chunk, 1), over_x)
+            self.go(chunk, 9, self.part(c, x, 1 - y, ALL, chunk), core)
         else:
-            self.copies[8 + half].wait_recv()
-            got = self.part(c, ALL, 1 - y, ALL, half) if half == 0 else self.part(c, 1 - x, ALL, ALL, half)
-        if step < 2:
-            over_x = (half == 0) == (step == 0)
-            to = device_at(c, 1 - x, y, z) if over_x else device_at(c, x, 1 - y, z)
-            self.go(6 + 2 * step + half, mine, to)
-        self.go(10 + 2 * step + half, got, device_at(1 - c, x, y, z))
-
-    def steps(self):
-        return [functools.partial(self.across, half, step) for step in range(3) for half in range(2)]
-
-    def finish(self):
-        for n in range(10, 16):
-            self.copies[n].wait_recv()
+            copies[chunk, 6].wait_recv()
+            copies[chunk, 8].wait_recv()
+            self.go(chunk, 10, self.part(c, 1 - x, 1 - y, ALL, chunk), core)
+
+    def arrived(self, chunk):
+        for n in (5, 7, 9, 10):
+            self.copies[chunk, n].wait_recv()
+
+    def drain(self):
         for copy in self.copies.values():
             copy.wait_send()
 
@@ -505,9 +525,9 @@
 def step_kernel(
     dims,
     len_ref, aux_ref, ids_ref, mask_ref, emb_ref, conv_ref, bias_ref, scorer_ref, cot_ref,
-    blocks_ref, loss_ref, embg_ref, convg_ref, biasg_ref, scoreg_ref,
-    taps_s, onehot_s, hidden_s, q_s, probs_s, similar_s, cot_s, band_s, pooled_s, hgrad_s,
-    blocks_s, part_s, conv_s, emb_s, convg_s,
+    blocks_ref, final_ref, sums_ref,
+    taps_s, onehot_s, hidden_s, q_s, probs_s, similar_s, cot_s, band_s, pooled_s, hgrad_s, matrix_s,
+    blocks_s, part_s, conv_s, emb_s,
     small_s, smalls_s, wcol_s, emball_s, tq_s, tqs_s, count_s, table_s,
     give_s, take_s, own_s, pass_s, came_s, zgive_s, zown_s, zcame_s, final_s, sums_s, sumr_s,
     local_sem, start_send, start_recv, half_sem, gather_send, gather_recv,
@@ -531,6 +551,7 @@
 
     mid = vocab // 2
     my_half = pl.ds(pl.multiple_of(c * mid, mid), mid)
+    my_rows = pl.ds(pl.multiple_of(x * (size // 2), size // 2), size // 2)
     my_tap, my_column = place_of(((c * 2 + x) * 2 + y) * 4 + z, TAPS, per_tap)
     local = [
         pltpu.make_async_copy(conv_ref, conv_s, local_sem.at[0]),
@@ -538,7 +559,7 @@
         pltpu.make_async_copy(
             conv_ref.at[my_tap, :, pl.ds(pl.multiple_of(my_column * 128, 128), 128)], wcol_s.at[f], local_sem.at[2]
         ),
-        pltpu.make_async_copy(emb_ref.at[my_half], emball_s.at[f, my_half], local_sem.at[3]),
+        pltpu.make_async_copy(emb_ref.at[my_rows, my_half], emball_s.at[f, my_rows, my_half], local_sem.at[3]),
     ]
     for r in range(rows):
         local.append(pltpu.make_async_copy(cot_ref.at[r], cot_s.at[r, pl.ds(EDGE, half)], local_sem.at[4 + r]))
@@ -558,20 +579,15 @@
         starts.append(remote(small_s, smalls_s.at[f], start_send.at[0, i], start_recv.at[0, i], peer))
         starts[-1].start()
     for i, peer in enumerate(peers):
-        tap, column = place_of(((c * 2 + x) * 2 + lax.rem(peer[0], 2)) * 4 + peer[0] // 2, TAPS, per_tap)
+        mine = emb_ref.at[my_rows, my_half]
         starts.append(
-            remote(emb_ref.at[my_half], emball_s.at[f, my_half], start_send.at[1, i], start_recv.at[1, i], peer)
+            remote(mine, emball_s.at[f, my_rows, my_half], start_send.at[1, i], start_recv.at[1, i], peer)
         )
         starts[-1].start()
-        starts.append(
-            remote(
-                conv_ref.at[tap, :, pl.ds(pl.multiple_of(column * 128, 128), 128)],
-                wcol_s.at[f],
-                start_send.at[2, i],
-                start_recv.at[2, i],
-                peer,
-            )
-        )
+    for i, peer in enumerate(peers):
+        tap, column = place_of(((c * 2 + x) * 2 + lax.rem(peer[0], 2)) * 4 + peer[0] // 2, TAPS, per_tap)
+        mine = conv_ref.at[tap, :, pl.ds(pl.multiple_of(column * 128, 128), 128)]
+        starts.append(remote(mine, wcol_s.at[f], start_send.at[2, i], start_recv.at[2, i], peer))
         starts[-1].start()
 
     fill_onehot(count, vocab, taps_s, onehot_s)
@@ -610,7 +626,7 @@
         axis=0,
     )
     u = jnp.concatenate(list(split3(u)) + [jnp.zeros((1, size), F32)], axis=0).astype(BF16)
-    tq = lax.dot_general(u, emb_s[...], across, preferred_element_type=F32)
+    tq = jnp.dot(u, emb_s[...], preferred_element_type=F32)
     tq_s[...] = jnp.zeros_like(tq_s)
     tq_s[0:TAPS, :] = tq[0:TAPS] + tq[TAPS : 2 * TAPS] + tq[2 * TAPS : 3 * TAPS]
     tqs_s[f] = tq_s[...]
@@ -623,21 +639,27 @@
     for copy in local[2:4]:
         copy.wait()
     for i in range(fs - 1):
-        starts[fs - 1 + 2 * i].wait_recv()
-    emb_core = remote(
-        emball_s.at[:, my_half], emball_s.at[:, my_half], half_sem.at[2], half_sem.at[3], core
-    )
+        starts[fs - 1 + i].wait_recv()
+    mine = emball_s.at[:, my_rows, my_half]
+    emb_x = remote(mine, mine, half_sem.at[6], half_sem.at[7], device_at(c, 1 - x, y, z))
+    emb_x.start()
+    emb_x.wait_recv()
+    mine = emball_s.at[:, :, my_half]
+    emb_core = remote(mine, mine, half_sem.at[2], half_sem.at[3], core)
     emb_core.start()
     for i in range(fs - 1):
-        starts[fs + 2 * i].wait_recv()
+        starts[2 * (fs - 1) + i].wait_recv()
     emb_core.wait_recv()
-    block = None
-    for g in range(fs):
-        term = lax.dot_general(wcol_s[g], emball_s[g], (((0,), (1,)), ((), ())), preferred_element_type=F32)
-        block = term if block is None else block + term
+    block = lax.dot_general(
+        wcol_s[...].reshape(fs * size, 128),
+        emball_s[...].reshape(fs * size, vocab),
+        (((0,), (0,)), ((), ())),
+        preferred_element_type=F32,
+    )
     table_s[c, x, y, z] = block.astype(BF16)
-    tables = Gather(table_s, me, gather_send.at[0], gather_recv.at[0])
-    tables.along_z()
+    tables = Gather(table_s, me, gather_send.at[0], gather_recv.at[0], TABLE_CHUNKS)
+    for chunk in range(TABLE_CHUNKS):
+        tables.along_z(chunk)
 
     count_x.wait_recv()
     count_s[2] = count_s[0] + count_s[1]
@@ -660,24 +682,56 @@
     fill_q(count, tq16, const, onehot_s, q_s)
     scores = block_scores(rows, length, m, q_s)
 
-    steps = tables.steps()
+    part = 128 // TABLE_CHUNKS
+
+    def table_rows(chunk):
+        return jnp.concatenate(
+            [
+                jnp.concatenate(
+                    [
+                        table_s[(*static_place(k, j, per_tap), slice(chunk * part, (chunk + 1) * part))]
+                        for j in range(per_tap)
+                    ],
+                    axis=0,
+                )
+                for k in range(TAPS)
+            ],
+            axis=1,
+        )
+
+    def hidden_part(chunk, low, high):
+        if low == 0:
+            tables.arrived(chunk)
+        bias_part = jnp.concatenate(
+            [bias_column[j * 128 + chunk * part : j * 128 + (chunk + 1) * part] for j in range(per_tap)], axis=0
+        )
+
+        def step(t, carry):
+            lanes = pl.ds(pl.multiple_of(t * TILE, TILE), TILE)
+            got = jnp.dot(table_rows(chunk), onehot_s[:, lanes], preferred_element_type=F32)
+            got = (got + bias_part).astype(BF16)
+            for j in range(per_tap):
+                hidden_s[j * 128 + chunk * part : j * 128 + (chunk + 1) * part, lanes] = got[
+                    j * part : (j + 1) * part
+                ]
+            return carry
+
+        lax.fori_loop(count * low // 4, count * high // 4, step, 0)
+
+    order = [(0, 0), (1, 0), (0, 1), (1, 1), (0, 2), (0, 0, 2), (1, 2), (0, 2, 4), (1, 0, 4)]
+    steps = [
+        functools.partial(tables.across if len(n) == 2 else hidden_part, *n) for n in order
+    ]
+    turns = {(0, 1): 1, (0, 3): 1, (1, 1): 1, (1, 3): 1}
 
     def between(r, t):
-        if steps and (r, t) != (0, 0):
+        for _ in range(turns.get((r, t), 0)):
             steps.pop(0)()
-
-    def whole(k):
-        return jnp.concatenate(
-            [table_s[static_place(k, j, per_tap)] for j in range(per_tap)], axis=0
-        )
 
     def late_hidden():
         while steps:
             steps.pop(0)()
-        tables.finish()
-        fill_hidden(
-            count, lambda: jnp.concatenate([whole(k) for k in range(TAPS)], axis=1), bias_column, onehot_s, hidden_s
-        )
+        tables.drain()
         for copy in local[4:]:
             copy.wait()
         count_c.wait_recv()
@@ -685,15 +739,8 @@
     def scale():
         return aux_ref[0, 0] / (count_s[2][0:1, 0:1] + count_s[3][0:1, 0:1])
 
-    refs = (hidden_s, cot_s, band_s, pooled_s, hgrad_s, probs_s, similar_s, blocks_s, part_s, late_hidden)
-    middle(dims[:4], m, scores, seg_list, real_list, scale, scorer, refs, between)
-    blocks_out = pltpu.make_async_copy(blocks_s, blocks_ref, local_sem.at[0])
-    blocks_out.start()
-
-    sums_s[0] = part_s[...]
-    sum_copies = [remote(sums_s.at[0], sumr_s.at[0], sum_send.at[0], sum_recv.at[0], core)]
-    sum_copies[0].start()
-
+    refs = (hidden_s, cot_s, band_s, pooled_s, hgrad_s, probs_s, similar_s, blocks_s, part_s, matrix_s, late_hidden)
+    pool = middle(dims[:4], m, scores, seg_list, real_list, scale, scorer, refs, between)
     def product(slot):
         tap, column = place_of(jnp.minimum(slot, TAPS * per_tap - 2), TAPS, per_tap)
         symbols = pl.ds(pl.multiple_of(tap * vocab, vocab), vocab)
@@ -703,109 +750,204 @@
     def core_copy(p):
         return remote(give_s.at[p], take_s.at[p], core_send.at[p], core_recv.at[p], core)
 
-    def give(p, carry):
+    def quad_of(t):
+        q = 3 - t // 2
+        qx, qy = lax.rem(x + q // 2, 2), lax.rem(y + lax.rem(q, 2), 2)
+        return qx, qy, qx * 4 + qy * 2 + lax.rem(t, 2)
+
+    def give(t):
+        p = quad_of(t)[2]
         give_s[p] = product((1 - c) * 16 + 2 * p)
         core_copy(p).start()
-        return carry
-
-    lax.fori_loop(0, 8, give, 0)
-
-    sum_copies[0].wait_recv()
-    sums_s[1] = sums_s[0] + sumr_s[0]
-    quad = [device_at(c, lax.rem(x + q // 2, 2), lax.rem(y + q % 2, 2), z) for q in range(4)]
-    for q in range(1, 4):
-        sum_copies.append(remote(sums_s.at[1], sumr_s.at[q], sum_send.at[q], sum_recv.at[q], quad[q]))
-        sum_copies[-1].start()
-
-    def quad_copy(t):
-        q = 3 - t // 2
-        to = device_at(c, lax.rem(x + q // 2, 2), lax.rem(y + lax.rem(q, 2), 2), z)
-        return remote(pass_s.at[t], came_s.at[t], quad_send.at[t], quad_recv.at[t], to)
-
-    def forward(t, carry):
-        q = 3 - t // 2
-        p = lax.rem(x + q // 2, 2) * 4 + lax.rem(y + lax.rem(q, 2), 2) * 2 + lax.rem(t, 2)
+
+    def keep(t):
+        p = quad_of(t)[2]
         got = product(c * 16 + 2 * p)
         core_copy(p).wait_recv()
-        pass_s[t] = (got + take_s[p]).astype(BF16)
-        quad_copy(t).start()
+        return got + take_s[p]
+
+    gap = vocab // GRAD_CHUNKS
+
+    def quad_copy(t, chunk):
+        qx, qy, _ = quad_of(t)
+        at = chunk * 6 + t
+        ref = t, pl.ds(chunk * gap, gap)
+        return remote(pass_s.at[ref], came_s.at[ref], quad_send.at[at], quad_recv.at[at], device_at(c, qx, qy, z))
+
+    def pass_on(t):
+        pass_s[t] = keep(t).astype(BF16)
+        for chunk in range(GRAD_CHUNKS):
+            quad_copy(t, chunk).start()
+
+    def forward(t, carry):
+        pass_on(t)
+        give(t + 2)
         return carry
 
+    give(jnp.int32(0))
+    give(jnp.int32(1))
     lax.fori_loop(0, 6, forward, 0)
-    for t in range(2):
-        p = x * 4 + y * 2 + t
-        got = product(c * 16 + 2 * p)
-        core_copy(p).wait_recv()
-        own_s[t] = got + take_s[p]
-
-    for q in range(1, 4):
-        sum_copies[q].wait_recv()
-    sums_s[2] = (sums_s[1] + sumr_s[1]) + (sumr_s[2] + sumr_s[3])
-    for i in range(1, 4):
-        to = device_at(c, x, y, lax.rem(z + i, 4))
-        sum_copies.append(remote(sums_s.at[2], sumr_s.at[3 + i], sum_send.at[3 + i], sum_recv.at[3 + i], to))
-        sum_copies[-1].start()
-
-    for t in range(2):
+    own_s[0] = keep(jnp.int32(6))
+    own_s[1] = keep(jnp.int32(7))
+
+    pool()
+    blocks_out = pltpu.make_async_copy(blocks_s, blocks_ref, local_sem.at[0])
+    blocks_out.start()
+    sums_s[0] = part_s[...]
+    sum_copies = [remote(sums_s.at[0], sumr_s.at[0], sum_send.at[0], sum_recv.at[0], core)]
+    sum_copies[0].start()
+
+    def sums_quad():
+        sum_copies[0].wait_recv()
+        sums_s[1] = sums_s[0] + sumr_s[0]
+        quad = [device_at(c, lax.rem(x + q // 2, 2), lax.rem(y + q % 2, 2), z) for q in range(4)]
         for q in range(1, 4):
-            quad_copy(6 - 2 * q + t).wait_recv()
-        total = own_s[t]
+            sum_copies.append(remote(sums_s.at[1], sumr_s.at[q], sum_send.at[q], sum_recv.at[q], quad[q]))
+            sum_copies[-1].start()
+
+    def sums_line():
         for q in range(1, 4):
-            total = total + came_s[6 - 2 * q + t].astype(F32)
-        for j in range(2):
-            zown_s[2 * t + j] = total[:, j * 128 : (j + 1) * 128]
-            zgive_s[2 * t + j] = total[:, j * 128 : (j + 1) * 128].astype(BF16)
-    line_copies = []
-    for i in range(1, 4):
-        to = lax.rem(z + i, 4)
-        copy = remote(
-            zgive_s.at[to], zcame_s.at[i - 1], line_send.at[i - 1], line_recv.at[i - 1], device_at(c, x, y, to)
-        )
-        copy.start()
-        line_copies.append(copy)
-    total = zown_s[z]
-    for i, copy in enumerate(line_copies):
-        copy.wait_recv()
-        total = total + zcame_s[i].astype(F32)
-    final_s[c, x, y, z] = total.astype(BF16)
-    grads = Gather(final_s, me, gather_send.at[1], gather_recv.at[1])
-    grads.along_z()
+            sum_copies[q].wait_recv()
+        sums_s[2] = (sums_s[1] + sumr_s[1]) + (sumr_s[2] + sumr_s[3])
+        for i in range(1, 4):
+            to = device_at(c, x, y, lax.rem(z + i, 4))
+            sum_copies.append(remote(sums_s.at[2], sumr_s.at[3 + i], sum_send.at[3 + i], sum_recv.at[3 + i], to))
+            sum_copies[-1].start()
+
+    grads = Gather(final_s, me, gather_send.at[1], gather_recv.at[1], GRAD_CHUNKS)
+    line_copies = {}
+
+    def to_line(chunk):
+        part = slice(chunk * gap, (chunk + 1) * gap)
+        for t in range(6):
+            quad_copy(jnp.int32(t), chunk).wait_recv()
+        for t in range(2):
+            total = own_s[t, part]
+            for q in range(1, 4):
+                total = total + came_s[6 - 2 * q + t, part].astype(F32)
+            for j in range(2):
+                zown_s[2 * t + j, part] = total[:, j * 128 : (j + 1) * 128]
+                zgive_s[2 * t + j, part] = total[:, j * 128 : (j + 1) * 128].astype(BF16)
+        for i in range(1, 4):
+            to = lax.rem(z + i, 4)
+            at = chunk * 3 + i - 1
+            part = pl.ds(chunk * gap, gap)
+            copy = remote(
+                zgive_s.at[to, part],
+                zcame_s.at[i - 1, part],
+                line_send.at[at],
+                line_recv.at[at],
+                device_at(c, x, y, to),
+            )
+            copy.start()
+            line_copies[chunk, i] = copy
+
+    def from_line(chunk):
+        part = slice(chunk * gap, (chunk + 1) * gap)
+        total = zown_s[z, part]
+        for i in range(1, 4):
+            line_copies[chunk, i].wait_recv()
+            total = total + zcame_s[i - 1, part].astype(F32)
+        final_s[c, x, y, z, part] = total.astype(BF16)
+        grads.along_z(chunk)
+
+    def put(chunk):
+        part = pl.ds(chunk * gap, gap)
+        ref = ALL, ALL, ALL, ALL, part
+        out_copies.append(pltpu.make_async_copy(final_s.at[ref], final_ref.at[ref], local_sem.at[1 + chunk]))
+        out_copies[-1].start()
+
+    out_copies = []
+    to_line(0)
+    sums_quad()
+    to_line(1)
+    from_line(0)
+    sums_line()
+    from_line(1)
+    grads.across(0, 0)
+    grads.across(1, 0)
+    grads.across(0, 1)
+    grads.across(1, 1)
+    grads.across(0, 2)
+    grads.across(1, 2)
+    grads.arrived(0)
+    put(0)
+    grads.arrived(1)
+    put(1)
+    grads.drain()
 
     for i in range(4, 7):
         sum_copies[i].wait_recv()
     sums = (sums_s[2] + sumr_s[4]) + (sumr_s[5] + sumr_s[6])
-    loss_ref[...] = sums[1:2, 0:1] / (count_s[2][0:1, 0:1] + count_s[3][0:1, 0:1])
-
-    for step in grads.steps():
-        step()
-    grads.finish()
+    total_count = count_s[2][0:1, 0:1] + count_s[3][0:1, 0:1]
+    sums_ref[...] = jnp.concatenate([sums[0:1], sums[1:2] / total_count, sums[2:8]], axis=0)
+
+    for copy in starts + tq_copies + sum_copies + list(line_copies.values()) + [count_x, count_c, emb_x, emb_core]:
+        copy.wait_send()
+    for p in range(8):
+        core_copy(p).wait_send()
+    for chunk in range(GRAD_CHUNKS):
+        for t in range(6):
+            quad_copy(jnp.int32(t), chunk).wait_send()
+    for copy in out_copies + [blocks_out]:
+        copy.wait()
+
+
+def last_kernel(
+    dims, blocks_ref, final_ref, sums_ref, emb_ref, conv_ref,
+    out_ref, loss_ref, embg_ref, convg_ref, biasg_ref, scoreg_ref,
+    blocks_s, final_s, emb_s, conv_s, convg_s, in_sem, out_sem,
+):
+    rows, length, width, vocab, size, fs = dims
+    per_tap = width // 128
+    copies = [
+        pltpu.make_async_copy(emb_ref, emb_s, in_sem.at[0]),
+        pltpu.make_async_copy(conv_ref, conv_s, in_sem.at[1]),
+    ]
+    for n in range(4):
+        copies.append(
+            pltpu.make_async_copy(final_ref.at[n // 2, n % 2], final_s.at[n // 2, n % 2], in_sem.at[2 + n])
+        )
+    blocks = [pltpu.make_async_copy(blocks_ref.at[r], blocks_s.at[r], in_sem.at[6 + r]) for r in range(rows)]
+    for copy in copies + blocks:
+        copy.start()
+    outs = []
+    have = 0
+    copies[0].wait()
+    copies[1].wait()
     emb_total = None
-    out_copies = []
     for k in range(TAPS):
+        while have * 8 < (k + 1) * per_tap:
+            copies[2 + have].wait()
+            have += 1
         grad = jnp.concatenate([final_s[static_place(k, j, per_tap)] for j in range(per_tap)], axis=1)
-        convg_s[k] = lax.dot_general(emb_s[...], grad, (((0,), (0,)), ((), ())), preferred_element_type=F32)
-        out_copies.append(pltpu.make_async_copy(convg_s.at[k], convg_ref.at[k], local_sem.at[1 + k]))
-        out_copies[-1].start()
-        term = lax.dot_general(grad, conv_s[k], across, preferred_element_type=F32)
+        convg_s[k] = jnp.dot(emb_s[...], grad, preferred_element_type=F32)
+        outs.append(pltpu.make_async_copy(convg_s.at[k], convg_ref.at[k], out_sem.at[k]))
+        outs[-1].start()
+        term = lax.dot_general(conv_s[k], grad, (((1,), (1,)), ((), ())), preferred_element_type=F32)
         emb_total = term if emb_total is None else emb_total + term
         if k == TAPS // 2:
             bias_line = jnp.sum(grad.astype(F32), axis=0, keepdims=True)
+        if k < rows:
+            blocks[k].wait()
+            outs.append(pltpu.make_async_copy(blocks_s.at[k], out_ref.at[k], out_sem.at[TAPS + k]))
+            outs[-1].start()
     embg_ref[...] = emb_total
+    f = lax.axis_index("fsdp")
+    lane = lax.broadcasted_iota(jnp.int32, (128, width), 0)
+    at = lax.broadcasted_iota(jnp.int32, (128, width), 1)
     pick = jnp.where((at == lane + f * size) & (lane < size), 1.0, 0.0).astype(BF16)
     lines = jnp.concatenate(
-        list(split3(bias_line)) + list(split3(sums[0:1])) + [jnp.zeros((10, width), F32)], axis=0
+        list(split3(bias_line)) + list(split3(sums_ref[0:1])) + [jnp.zeros((10, width), F32)], axis=0
     ).astype(BF16)
-    mine = lax.dot_general(lines, pick, across, preferred_element_type=F32)
+    mine = lax.dot_general(lines, pick, (((1,), (1,)), ((), ())), preferred_element_type=F32)
     biasg_ref[...] = (mine[0:1] + mine[1:2] + mine[2:3])[:, :size]
     scoreg_ref[...] = (mine[3:4] + mine[4:5] + mine[5:6])[:, :size]
-
-    for copy in starts + tq_copies + sum_copies + line_copies + [count_x, count_c, emb_core]:
-        copy.wait_send()
-    for p in range(8):
-        core_copy(p).wait_send()
-    for t in range(6):
-        quad_copy(t).wait_send()
-    for copy in out_copies + [blocks_out]:
+    loss_ref[...] = sums_ref[1:2, 0:1]
+    while have < 4:
+        copies[2 + have].wait()
+        have += 1
+    for copy in outs:
         copy.wait()
 
 
@@ -820,29 +962,25 @@
     smem = pl.BlockSpec(memory_space=pltpu.SMEM)
     hbm = pl.BlockSpec(memory_space=pl.ANY)
     dma = pltpu.SemaphoreType.DMA
-    blocks, loss, emb_grad, conv_grad, bias_grad, score_grad = pl.pallas_call(
+    blocks, final, sums = pl.pallas_call(
         functools.partial(step_kernel, dims),
         out_shape=(
             jax.ShapeDtypeStruct((rows, half, width), BF16),
-            jax.ShapeDtypeStruct((1, 1), F32),
-            jax.ShapeDtypeStruct((vocab, size), F32),
-            jax.ShapeDtypeStruct((TAPS, size, width), F32),
-            jax.ShapeDtypeStruct((1, size), F32),
-            jax.ShapeDtypeStruct((1, size), F32),
+            jax.ShapeDtypeStruct((2, 2, 2, 4, vocab, 128), BF16),
+            jax.ShapeDtypeStruct((8, width), F32),
         ),
         in_specs=[smem, smem, vmem, vmem, hbm, hbm, vmem, vmem, hbm],
-        out_specs=(hbm, vmem, vmem, hbm, vmem, vmem),
+        out_specs=(hbm, hbm, vmem),
         scratch_shapes=local_scratch(rows, length, width, vocab)
         + [
             pltpu.VMEM((rows, half, width), BF16),
             pltpu.VMEM((8, width), F32),
             pltpu.VMEM((TAPS, size, width), BF16),
-            pltpu.VMEM((vocab, size), BF16),
-            pltpu.VMEM((TAPS, size, width), F32),
+            pltpu.VMEM((size, vocab), BF16),
             pltpu.VMEM((8, 128), F32),
             pltpu.VMEM((fs, 8, 128), F32),
             pltpu.VMEM((fs, size, 128), BF16),
-            pltpu.VMEM((fs, vocab, size), BF16),
+            pltpu.VMEM((fs, size, vocab), BF16),
             pltpu.VMEM((8, vocab), F32),
             pltpu.VMEM((fs, 8, vocab), F32),
             pltpu.VMEM((4, 8, 128), F32),
@@ -861,15 +999,15 @@
             dma((4 + max(rows, 2),)),
             dma((4, fs - 1)),
             dma((4, fs - 1)),
-            dma((6,)),
-            dma((2, 16)),
-            dma((2, 16)),
+            dma((8,)),
+            dma((2, 11 * max(TABLE_CHUNKS, GRAD_CHUNKS))),
+            dma((2, 11 * max(TABLE_CHUNKS, GRAD_CHUNKS))),
             dma((8,)),
             dma((8,)),
-            dma((6,)),
-            dma((6,)),
-            dma((3,)),
-            dma((3,)),
+            dma((6 * GRAD_CHUNKS,)),
+            dma((6 * GRAD_CHUNKS,)),
+            dma((3 * GRAD_CHUNKS,)),
+            dma((3 * GRAD_CHUNKS,)),
             dma((7,)),
             dma((7,)),
         ],
@@ -882,13 +1020,37 @@
         aux_weight.reshape(1, 1),
         byte_ids,
         pad_mask,
-        embedding,
+        embedding.T,
         conv_weight,
         conv_bias.reshape(1, size),
         scorer.reshape(1, size),
         cotangent,
     )
-    return blocks, loss.reshape(()), emb_grad, conv_grad, bias_grad.reshape(size), score_grad.reshape(size)
+    blocks, loss, emb_grad, conv_grad, bias_grad, score_grad = pl.pallas_call(
+        functools.partial(last_kernel, dims),
+        out_shape=(
+            jax.ShapeDtypeStruct((rows, half, width), BF16),
+            jax.ShapeDtypeStruct((1, 1), F32),
+            jax.ShapeDtypeStruct((size, vocab), F32),
+            jax.ShapeDtypeStruct((TAPS, size, width), F32),
+            jax.ShapeDtypeStruct((1, size), F32),
+            jax.ShapeDtypeStruct((1, size), F32),
+        ),
+        in_specs=[hbm, hbm, vmem, hbm, hbm],
+        out_specs=(hbm, vmem, vmem, hbm, vmem, vmem),
+        scratch_shapes=[
+            pltpu.VMEM((rows, half, width), BF16),
+            pltpu.VMEM((2, 2, 2, 4, vocab, 128), BF16),
+            pltpu.VMEM((size, vocab), BF16),
+            pltpu.VMEM((TAPS, size, width), BF16),
+            pltpu.VMEM((TAPS, size, width), F32),
+            dma((6 + rows,)),
+            dma((rows + TAPS,)),
+        ],
+        compiler_params=pltpu.CompilerParams(vmem_limit_bytes=62 * 1024 * 1024),
+        name="last",
+    )(blocks, final, sums, embedding.T, conv_weight)
+    return blocks, loss.reshape(()), emb_grad.T, conv_grad, bias_grad.reshape(size), score_grad.reshape(size)
 
 
 def split3_rows(x):

time: 113 us -> 95.2 us (0.84)
  Pallas kernels: 101 us -> 92.9 us
  local copies, waits for them, and re-layouts: 8.08 us -> 0 us
  between operations: 3.11 us -> 1.45 us
    pallas_call x1, Pallas kernels: 101 us -> 87.4 us  [step_shards(): pl.pallas_call(functools.partial(step_kernel, dims), out_shape=(jax.Shape...]
    unnamed x12 -> x0, local copies, waits for them, and re-layouts: 8.08 us -> none
    pallas_call x0 -> x1, Pallas kernels: none -> 5.52 us  [step_shards(): pl.pallas_call(functools.partial(last_kernel, dims), out_shape=(jax.Shape...]
where the time goes in v2:
time: 95.2 us; the launch traced here: 94.4 us
  Pallas kernels  92.9 us (98%)
  between operations  1.45 us (2%)
    pallas_call x1, Pallas kernels, step_shards(): pl.pallas_call(functools.partial(step_kernel, dims), out_shape=(jax.Shape...  87.4 us
    pallas_call x1, Pallas kernels, step_shards(): pl.pallas_call(functools.partial(last_kernel, dims), out_shape=(jax.Shape...  5.52 us

profile of v2, /device:TPU:1, one launch (start us, length us, event | category | flops | bytes accessed | tf_op | source)
XLA Modules:
  0.0 94.4 jit_solution(17870014219225347459)
XLA Ops:
  1.3 87.4 %step.1 = (bf16[2,512,768]{2,1,0:T(8,128)(2,1)}, bf16[2,2,2,4,256,128]{5,4,3,2,1,0:T(8,128)(2,1)}, f32[8,768]{1,0:T(8,128)}) custom-call(s32[2,8]{1,0:T(2,128)} %len_ref.1, f32[1,1]{1,0:T(1,128)} %bitcast.8.aux_ref, s32[2,1024]{1,0:T(2,128)} %ids_ref.1, s32[2,1024]{1,0:T(2,128)} %mask_ref.1, bf16[96,256]{1,0:T(8,128)(2,1)} %bitcast.9, ...), custom_call_target="tpu_custom_call" | custom-call | tf_op jit(solution)/shard_map/step/pallas_call | solution.py:965
  88.7 5.5 %last.1 = (bf16[2,512,768]{2,1,0:T(8,128)(2,1)}, f32[1,1]{1,0:T(1,128)}, f32[96,256]{1,0:T(8,128)}, f32[5,96,768]{2,1,0:T(8,128)}, f32[1,96]{1,0:T(1,128)}, /*index=5*/f32[1,96]{1,0:T(1,128)}) custom-call(bf16[2,512,768]{2,1,0:T(8,128)(2,1)} %get-tuple-element.15.blocks_ref, bf16[2,2,2,4,256,128]{5,4,3,2,1,0:T(8,128)(2,1)} %get-tuple-element.16.final_ref, ...), custom_call_target="tpu_custom_call" | custom-call | tf_op jit(solution)/shard_map/last/pallas_call | solution.py:1029

commit v3 on v2

--- a/solution.py
+++ b/solution.py
@@ -185,10 +185,7 @@
     return weight, log_weight, entropy
 
 
-def band_products(rows, length, cot_s, hidden_s, band_s, window):
-    kl = lax.broadcasted_iota(jnp.int32, (window, TILE), 0)
-    jl = lax.broadcasted_iota(jnp.int32, (window, TILE), 1) // 2 + EDGE
-    diagonal = kl - jl
+def band_products(rows, length, cot_s, hidden_s, band_s, window, diagonal):
     for r in range(rows):
         for t in range(length // TILE):
             lanes = slice(r * length + t * TILE, r * length + (t + 1) * TILE)
@@ -198,7 +195,6 @@
             )
             for d in range(-2, 3):
                 band_s[d + 2 : d + 3, lanes] = jnp.sum(jnp.where(diagonal == d, prod, 0.0), axis=0, keepdims=True)
-    return diagonal
 
 
 def calibrate_back(r, length, scores, cal_grad, inner, moments, norm, probs_s):
@@ -260,8 +256,29 @@
     for r in range(rows):
         pooled_s[r] = jnp.zeros_like(pooled_s[r])
 
+    use = pair_weight * weight * inverse
+    moved = {o: (use if o == 0 else same[o] * shift(use, o)) for o in range(1 - SIZES, SIZES)}
+    mix = []
+    for d in range(-2, 3):
+        odd_sum = sum([moved[o] for o in moved if DELTA_ODD[o] == d], jnp.zeros_like(use))
+        even_sum = sum([moved[o] for o in moved if DELTA_EVEN[o] == d], jnp.zeros_like(use))
+        mix.append(group_all(jnp.where(m["even"], even_sum, odd_sum) * real, jnp.add, bits))
+
+    kl = lax.broadcasted_iota(jnp.int32, (window, TILE), 0)
+    diagonal = kl - (lax.broadcasted_iota(jnp.int32, (window, TILE), 1) // 2 + EDGE)
+    for r in range(rows):
+        at = r * SIZES
+        for t in range(tiles):
+            lanes = slice(t * TILE, (t + 1) * TILE)
+            matrix = jnp.zeros((window, TILE), F32)
+            for d in range(-2, 3):
+                matrix = jnp.where(diagonal == d, mix[d + 2][at : at + 1, lanes], matrix)
+            high, low = split2(matrix)
+            matrix_s[r * tiles + t, 0:window] = high.astype(BF16)
+            matrix_s[r * tiles + t, window : 2 * window] = low.astype(BF16)
+
     late_hidden()
-    diagonal = band_products(rows, length, cot_s, hidden_s, band_s, window)
+    band_products(rows, length, cot_s, hidden_s, band_s, window, diagonal)
     even1 = (lax.broadcasted_iota(jnp.int32, (1, length), 1) & 1) == 0
     band = [[lane_rows(band_s, d + 2, r, length) for d in range(-2, 3)] for r in range(rows)]
 
@@ -287,14 +304,6 @@
         q_grad = q_grad + same[o] * shift(score_grad, o)
     q_grad = group_all(q_grad * real, jnp.add, bits)
 
-    use = pair_weight * weight * inverse
-    moved = {o: (use if o == 0 else same[o] * shift(use, o)) for o in range(1 - SIZES, SIZES)}
-    mix = []
-    for d in range(-2, 3):
-        odd_sum = sum([moved[o] for o in moved if DELTA_ODD[o] == d], jnp.zeros_like(use))
-        even_sum = sum([moved[o] for o in moved if DELTA_EVEN[o] == d], jnp.zeros_like(use))
-        mix.append(group_all(jnp.where(m["even"], even_sum, odd_sum) * real, jnp.add, bits))
-
     scorer16 = jnp.concatenate([scorer, scorer, jnp.zeros((EDGE - 2, width), BF16)], axis=0)
     for r in range(rows):
         at = r * SIZES
@@ -303,18 +312,13 @@
             lanes = slice(t * TILE, (t + 1) * TILE)
             all_lanes = slice(r * length + t * TILE, r * length + (t + 1) * TILE)
             first = t * TILE // 2
-            matrix = jnp.zeros((window, TILE), F32)
-            for d in range(-2, 3):
-                matrix = jnp.where(diagonal == d, mix[d + 2][at : at + 1, lanes], matrix)
-            high, low = split2(matrix)
-            matrix = jnp.concatenate(
-                [high, low, q_high[:, lanes], q_low[:, lanes], jnp.zeros((EDGE - 2, TILE), F32)], axis=0
+            matrix_s[r * tiles + t, 2 * window :] = jnp.concatenate(
+                [q_high[:, lanes], q_low[:, lanes], jnp.zeros((EDGE - 2, TILE), F32)], axis=0
             ).astype(BF16)
-            matrix_s[r * tiles + t] = matrix
             here = cot_s[r, first : first + window, :]
             given = jnp.concatenate([here, here, scorer16], axis=0)
             hgrad_s[all_lanes, :] = lax.dot_general(
-                matrix, given, (((0,), (0,)), ((), ())), preferred_element_type=F32
+                matrix_s[r * tiles + t], given, (((0,), (0,)), ((), ())), preferred_element_type=F32
             ).astype(BF16)
 
     def pool():
@@ -524,14 +528,15 @@
 
 def step_kernel(
     dims,
-    len_ref, aux_ref, ids_ref, mask_ref, emb_ref, conv_ref, bias_ref, scorer_ref, cot_ref,
-    blocks_ref, final_ref, sums_ref,
+    len_in, aux_in, ids_in, mask_in, emb_ref, conv_ref, bias_in, scorer_in, cot_ref,
+    blocks_ref, final_ref, sums_out,
     taps_s, onehot_s, hidden_s, q_s, probs_s, similar_s, cot_s, band_s, pooled_s, hgrad_s, matrix_s,
     blocks_s, part_s, conv_s, emb_s,
     small_s, smalls_s, wcol_s, emball_s, tq_s, tqs_s, count_s, table_s,
     give_s, take_s, own_s, pass_s, came_s, zgive_s, zown_s, zcame_s, final_s, sums_s, sumr_s,
     local_sem, start_send, start_recv, half_sem, gather_send, gather_recv,
     core_send, core_recv, quad_send, quad_recv, line_send, line_recv, sum_send, sum_recv,
+    len_ref, aux_ref, ids_ref, mask_ref, bias_ref, scorer_ref, sums_ref, in_sem,
 ):
     rows, length, width, vocab, size, fs = dims
     half = length // 2
@@ -549,6 +554,21 @@
     for peer in peers + others:
         pl.semaphore_signal(barrier, inc=1, device_id=peer, device_id_type=MESH)
 
+    inputs = [
+        pltpu.make_async_copy(source, target, in_sem.at[n])
+        for n, (source, target) in enumerate(
+            [
+                (len_in, len_ref),
+                (ids_in, ids_ref),
+                (mask_in, mask_ref),
+                (bias_in, bias_ref),
+                (scorer_in, scorer_ref),
+                (aux_in, aux_ref),
+            ]
+        )
+    ]
+    for copy in inputs:
+        copy.start()
     mid = vocab // 2
     my_half = pl.ds(pl.multiple_of(c * mid, mid), mid)
     my_rows = pl.ds(pl.multiple_of(x * (size // 2), size // 2), size // 2)
@@ -565,6 +585,8 @@
         local.append(pltpu.make_async_copy(cot_ref.at[r], cot_s.at[r, pl.ds(EDGE, half)], local_sem.at[4 + r]))
     for copy in local:
         copy.start()
+    for copy in inputs:
+        copy.wait()
     real_here = jnp.sum(jnp.sum(mask_ref[...].astype(F32), axis=1, keepdims=True), axis=0, keepdims=True)
     small_s[...] = jnp.zeros_like(small_s)
     small_s[0:1, 0:size] = bias_ref[...].astype(F32)
@@ -881,6 +903,8 @@
     sums = (sums_s[2] + sumr_s[4]) + (sumr_s[5] + sumr_s[6])
     total_count = count_s[2][0:1, 0:1] + count_s[3][0:1, 0:1]
     sums_ref[...] = jnp.concatenate([sums[0:1], sums[1:2] / total_count, sums[2:8]], axis=0)
+    out_copies.append(pltpu.make_async_copy(sums_ref, sums_out, in_sem.at[0]))
+    out_copies[-1].start()
 
     for copy in starts + tq_copies + sum_copies + list(line_copies.values()) + [count_x, count_c, emb_x, emb_core]:
         copy.wait_send()
@@ -894,9 +918,10 @@
 
 
 def last_kernel(
-    dims, blocks_ref, final_ref, sums_ref, emb_ref, conv_ref,
-    out_ref, loss_ref, embg_ref, convg_ref, biasg_ref, scoreg_ref,
+    dims, blocks_ref, final_ref, sums_in, emb_ref, conv_ref,
+    out_ref, loss_out, embg_out, convg_ref, biasg_out, scoreg_out,
     blocks_s, final_s, emb_s, conv_s, convg_s, in_sem, out_sem,
+    sums_ref, loss_ref, embg_ref, biasg_ref, scoreg_ref,
 ):
     rows, length, width, vocab, size, fs = dims
     per_tap = width // 128
@@ -909,6 +934,7 @@
             pltpu.make_async_copy(final_ref.at[n // 2, n % 2], final_s.at[n // 2, n % 2], in_sem.at[2 + n])
         )
     blocks = [pltpu.make_async_copy(blocks_ref.at[r], blocks_s.at[r], in_sem.at[6 + r]) for r in range(rows)]
+    copies.append(pltpu.make_async_copy(sums_in, sums_ref, in_sem.at[6 + rows]))
     for copy in copies + blocks:
         copy.start()
     outs = []
@@ -933,6 +959,7 @@
             outs.append(pltpu.make_async_copy(blocks_s.at[k], out_ref.at[k], out_sem.at[TAPS + k]))
             outs[-1].start()
     embg_ref[...] = emb_total
+    copies[6].wait()
     f = lax.axis_index("fsdp")
     lane = lax.broadcasted_iota(jnp.int32, (128, width), 0)
     at = lax.broadcasted_iota(jnp.int32, (128, width), 1)
@@ -944,6 +971,11 @@
     biasg_ref[...] = (mine[0:1] + mine[1:2] + mine[2:3])[:, :size]
     scoreg_ref[...] = (mine[3:4] + mine[4:5] + mine[5:6])[:, :size]
     loss_ref[...] = sums_ref[1:2, 0:1]
+    for n, (source, target) in enumerate(
+        [(embg_ref, embg_out), (biasg_ref, biasg_out), (scoreg_ref, scoreg_out), (loss_ref, loss_out)]
+    ):
+        outs.append(pltpu.make_async_copy(source, target, out_sem.at[TAPS + rows + n]))
+        outs[-1].start()
     while have < 4:
         copies[2 + have].wait()
         have += 1
@@ -958,8 +990,6 @@
     half = length // 2
     fs = width // size
     dims = (rows, length, width, vocab, size, fs)
-    vmem = pl.BlockSpec(memory_space=pltpu.VMEM)
-    smem = pl.BlockSpec(memory_space=pltpu.SMEM)
     hbm = pl.BlockSpec(memory_space=pl.ANY)
     dma = pltpu.SemaphoreType.DMA
     blocks, final, sums = pl.pallas_call(
@@ -969,8 +999,8 @@
             jax.ShapeDtypeStruct((2, 2, 2, 4, vocab, 128), BF16),
             jax.ShapeDtypeStruct((8, width), F32),
         ),
-        in_specs=[smem, smem, vmem, vmem, hbm, hbm, vmem, vmem, hbm],
-        out_specs=(hbm, hbm, vmem),
+        in_specs=[hbm] * 9,
+        out_specs=(hbm, hbm, hbm),
         scratch_shapes=local_scratch(rows, length, width, vocab)
         + [
             pltpu.VMEM((rows, half, width), BF16),
@@ -1010,6 +1040,14 @@
             dma((3 * GRAD_CHUNKS,)),
             dma((7,)),
             dma((7,)),
+            pltpu.SMEM(doc_lengths.shape, jnp.int32),
+            pltpu.SMEM((1, 1), F32),
+            pltpu.VMEM((rows, length), jnp.int32),
+            pltpu.VMEM((rows, length), jnp.int32),
+            pltpu.VMEM((1, size), BF16),
+            pltpu.VMEM((1, size), BF16),
+            pltpu.VMEM((8, width), F32),
+            dma((6,)),
         ],
         compiler_params=pltpu.CompilerParams(
             collective_id=0, has_side_effects=True, vmem_limit_bytes=62 * 1024 * 1024
@@ -1036,16 +1074,21 @@
             jax.ShapeDtypeStruct((1, size), F32),
             jax.ShapeDtypeStruct((1, size), F32),
         ),
-        in_specs=[hbm, hbm, vmem, hbm, hbm],
-        out_specs=(hbm, vmem, vmem, hbm, vmem, vmem),
+        in_specs=[hbm] * 5,
+        out_specs=(hbm,) * 6,
         scratch_shapes=[
             pltpu.VMEM((rows, half, width), BF16),
             pltpu.VMEM((2, 2, 2, 4, vocab, 128), BF16),
             pltpu.VMEM((size, vocab), BF16),
             pltpu.VMEM((TAPS, size, width), BF16),
             pltpu.VMEM((TAPS, size, width), F32),
-            dma((6 + rows,)),
-            dma((rows + TAPS,)),
+            dma((7 + rows,)),
+            dma((rows + TAPS + 4,)),
+            pltpu.VMEM((8, width), F32),
+            pltpu.VMEM((1, 1), F32),
+            pltpu.VMEM((size, vocab), F32),
+            pltpu.VMEM((1, size), F32),
+            pltpu.VMEM((1, size), F32),
         ],
         compiler_params=pltpu.CompilerParams(vmem_limit_bytes=62 * 1024 * 1024),
         name="last",

time: 95.2 us -> 91.9 us (0.965)
  Pallas kernels: 92.9 us -> 90.2 us
    pallas_call x1, Pallas kernels: 87.4 us -> 85.9 us  [step_shards(): pl.pallas_call(functools.partial(step_kernel, dims), out_shape=(jax.Shape...]
    pallas_call x1, Pallas kernels: 5.52 us -> 4.29 us  [step_shards(): pl.pallas_call(functools.partial(last_kernel, dims), out_shape=(jax.Shape...]
where the time goes in v3:
time: 91.9 us; the launch traced here: 91.7 us
  Pallas kernels  90.2 us (98%)
  between operations  1.45 us (2%)
    pallas_call x1, Pallas kernels, step_shards(): pl.pallas_call(functools.partial(step_kernel, dims), out_shape=(jax.Shape...  85.9 us
    pallas_call x1, Pallas kernels, step_shards(): pl.pallas_call(functools.partial(last_kernel, dims), out_shape=(jax.Shape...  4.29 us

profile of v3, /device:TPU:1, one launch (start us, length us, event | category | flops | bytes accessed | tf_op | source)
XLA Modules:
  0.0 91.7 jit_solution(15209890109543596834)
XLA Ops:
  1.3 85.9 %step.1 = (bf16[2,512,768]{2,1,0:T(8,128)(2,1)}, bf16[2,2,2,4,256,128]{5,4,3,2,1,0:T(8,128)(2,1)}, f32[8,768]{1,0:T(8,128)}) custom-call(s32[2,8]{1,0:T(2,128)} %len_in.1, f32[1,1]{1,0:T(1,128)} %bitcast.8.aux_in, s32[2,1024]{1,0:T(2,128)} %ids_in.1, s32[2,1024]{1,0:T(2,128)} %mask_in.1, bf16[96,256]{1,0:T(8,128)(2,1)} %bitcast.9, ...), custom_call_target="tpu_custom_call" | custom-call | tf_op jit(solution)/shard_map/step/pallas_call | solution.py:995
  87.2 4.3 %last.1 = (bf16[2,512,768]{2,1,0:T(8,128)(2,1)}, f32[1,1]{1,0:T(1,128)}, f32[96,256]{1,0:T(8,128)}, f32[5,96,768]{2,1,0:T(8,128)}, f32[1,96]{1,0:T(1,128)}, /*index=5*/f32[1,96]{1,0:T(1,128)}) custom-call(bf16[2,512,768]{2,1,0:T(8,128)(2,1)} %get-tuple-element.15.blocks_ref, bf16[2,2,2,4,256,128]{5,4,3,2,1,0:T(8,128)(2,1)} %get-tuple-element.16.final_ref, ...), custom_call_target="tpu_custom_call" | custom-call | tf_op jit(solution)/shard_map/last/pallas_call | solution.py:1067

commit v4 on v3

--- a/solution.py
+++ b/solution.py
@@ -722,7 +722,7 @@
         )
 
     def hidden_part(chunk, low, high):
-        if low == 0:
+        if low == 0 and chunk < TABLE_CHUNKS - 1:
             tables.arrived(chunk)
         bias_part = jnp.concatenate(
             [bias_column[j * 128 + chunk * part : j * 128 + (chunk + 1) * part] for j in range(per_tap)], axis=0
@@ -738,7 +738,8 @@
                 ]
             return carry
 
-        lax.fori_loop(count * low // 4, count * high // 4, step, 0)
+        for t in range(count * low // 4, count * high // 4):
+            step(t, 0)
 
     order = [(0, 0), (1, 0), (0, 1), (1, 1), (0, 2), (0, 0, 2), (1, 2), (0, 2, 4), (1, 0, 4)]
     steps = [
@@ -751,12 +752,14 @@
             steps.pop(0)()
 
     def late_hidden():
-        while steps:
+        while len(steps) > 1:
             steps.pop(0)()
+        tables.arrived(TABLE_CHUNKS - 1)
         tables.drain()
         for copy in local[4:]:
             copy.wait()
         count_c.wait_recv()
+        steps.pop(0)()
 
     def scale():
         return aux_ref[0, 0] / (count_s[2][0:1, 0:1] + count_s[3][0:1, 0:1])
@@ -881,12 +884,12 @@
 
     out_copies = []
     to_line(0)
-    sums_quad()
     to_line(1)
     from_line(0)
+    from_line(1)
+    sums_quad()
+    grads.across(0, 0)
     sums_line()
-    from_line(1)
-    grads.across(0, 0)
     grads.across(1, 0)
     grads.across(0, 1)
     grads.across(1, 1)

time: 91.9 us -> 88.9 us (0.967)
  Pallas kernels: 90.2 us -> 87.3 us
    pallas_call x1, Pallas kernels: 85.9 us -> 83 us  [step_shards(): pl.pallas_call(functools.partial(step_kernel, dims), out_shape=(jax.Shape...]
where the time goes in v4:
time: 88.9 us; the launch traced here: 88.8 us
  Pallas kernels  87.3 us (98%)
  between operations  1.45 us (2%)
    pallas_call x1, Pallas kernels, step_shards(): pl.pallas_call(functools.partial(step_kernel, dims), out_shape=(jax.Shape...  83 us
    pallas_call x1, Pallas kernels, step_shards(): pl.pallas_call(functools.partial(last_kernel, dims), out_shape=(jax.Shape...  4.29 us

profile of v4, /device:TPU:1, one launch (start us, length us, event | category | flops | bytes accessed | tf_op | source)
XLA Modules:
  0.0 88.8 jit_solution(350654425257769708)
XLA Ops:
  1.3 83.0 %step.1 = (bf16[2,512,768]{2,1,0:T(8,128)(2,1)}, bf16[2,2,2,4,256,128]{5,4,3,2,1,0:T(8,128)(2,1)}, f32[8,768]{1,0:T(8,128)}) custom-call(s32[2,8]{1,0:T(2,128)} %len_in.1, f32[1,1]{1,0:T(1,128)} %bitcast.8.aux_in, s32[2,1024]{1,0:T(2,128)} %ids_in.1, s32[2,1024]{1,0:T(2,128)} %mask_in.1, bf16[96,256]{1,0:T(8,128)(2,1)} %bitcast.9, ...), custom_call_target="tpu_custom_call" | custom-call | tf_op jit(solution)/shard_map/step/pallas_call | solution.py:998
  84.3 4.3 %last.1 = (bf16[2,512,768]{2,1,0:T(8,128)(2,1)}, f32[1,1]{1,0:T(1,128)}, f32[96,256]{1,0:T(8,128)}, f32[5,96,768]{2,1,0:T(8,128)}, f32[1,96]{1,0:T(1,128)}, /*index=5*/f32[1,96]{1,0:T(1,128)}) custom-call(bf16[2,512,768]{2,1,0:T(8,128)(2,1)} %get-tuple-element.15.blocks_ref, bf16[2,2,2,4,256,128]{5,4,3,2,1,0:T(8,128)(2,1)} %get-tuple-element.16.final_ref, ...), custom_call_target="tpu_custom_call" | custom-call | tf_op jit(solution)/shard_map/last/pallas_call | solution.py:1070

commit v5 on v4

--- a/solution.py
+++ b/solution.py
@@ -132,6 +132,14 @@
     return total * m["inverse"]
 
 
+def near_keys(t, length):
+    return [
+        j
+        for j in range(length // 128)
+        if max(j * 128 - (t * TILE + TILE - 1), t * TILE - (j * 128 + 127)) < length // 2
+    ]
+
+
 def calibrate_row(r, length, scores, seg, real, similar_s, probs_s, between):
     s = scores[r * SIZES : (r + 1) * SIZES]
     a, rest = split2(s)
@@ -154,7 +162,8 @@
         lanes = slice(t * TILE, (t + 1) * TILE)
         query_seg = seg[:, lanes]
         top = None
-        for j in range(length // 128):
+        near = near_keys(t, length)
+        for j in near:
             keys = slice(j * 128, (j + 1) * 128)
             sim = jnp.dot(left[keys], right[:, lanes], preferred_element_type=F32)
             allowed = key_column[keys] == query_seg
@@ -166,10 +175,11 @@
             similar_s[keys, :] = sim
             here = jnp.max(sim, axis=0, keepdims=True)
             top = here if top is None else jnp.maximum(top, here)
-        for j in range(length // 128):
+        for j in near:
             keys = slice(j * 128, (j + 1) * 128)
             probs_s[r, keys, lanes] = jnp.exp(similar_s[keys, :] - top).astype(BF16)
-        outs.append(jnp.dot(features, probs_s[r, :, lanes], preferred_element_type=F32))
+        keys = slice(near[0] * 128, (near[-1] + 1) * 128)
+        outs.append(jnp.dot(features[:, keys], probs_s[r, keys, lanes], preferred_element_type=F32))
         between(r, t)
     moments = jnp.concatenate(outs, axis=1)
     moments = moments[0:16] + moments[16:32]
@@ -220,7 +230,12 @@
     for t in range(length // TILE):
         keys = slice(t * TILE, (t + 1) * TILE)
         outs.append(
-            lax.dot_general(features, probs_s[r, keys, :], (((1,), (1,)), ((), ())), preferred_element_type=F32)
+            lax.dot_general(
+                features[:, max(t - 2, 0) * TILE : (t + 3) * TILE],
+                probs_s[r, keys, max(t - 2, 0) * TILE : min(t + 3, length // TILE) * TILE],
+                (((1,), (1,)), ((), ())),
+                preferred_element_type=F32,
+            )
         )
     back = jnp.concatenate(outs, axis=1)
     back = back[0:24] + back[24:48]
@@ -533,7 +548,7 @@
     taps_s, onehot_s, hidden_s, q_s, probs_s, similar_s, cot_s, band_s, pooled_s, hgrad_s, matrix_s,
     blocks_s, part_s, conv_s, emb_s,
     small_s, smalls_s, wcol_s, emball_s, tq_s, tqs_s, count_s, table_s,
-    give_s, take_s, own_s, pass_s, came_s, zgive_s, zown_s, zcame_s, final_s, sums_s, sumr_s,
+    give_s, take_s, own_s, hold_s, pass_s, came_s, zgive_s, zown_s, zcame_s, final_s, sums_s, sumr_s,
     local_sem, start_send, start_recv, half_sem, gather_send, gather_recv,
     core_send, core_recv, quad_send, quad_recv, line_send, line_recv, sum_send, sum_recv,
     len_ref, aux_ref, ids_ref, mask_ref, bias_ref, scorer_ref, sums_ref, in_sem,
@@ -615,6 +630,14 @@
     fill_onehot(count, vocab, taps_s, onehot_s)
     cot_s[:, 0:EDGE, :] = jnp.zeros((rows, EDGE, width), BF16)
     cot_s[:, EDGE + half :, :] = jnp.zeros((rows, EDGE, width), BF16)
+
+    for copy in local[2:4]:
+        copy.wait()
+    for i in range(fs - 1):
+        starts[fs - 1 + i].wait_recv()
+    mine = emball_s.at[:, my_rows, my_half]
+    emb_x = remote(mine, mine, half_sem.at[6], half_sem.at[7], device_at(c, 1 - x, y, z))
+    emb_x.start()
 
     for i in range(fs - 1):
         starts[i].wait_recv()
@@ -658,13 +681,6 @@
         copy.start()
         tq_copies.append(copy)
 
-    for copy in local[2:4]:
-        copy.wait()
-    for i in range(fs - 1):
-        starts[fs - 1 + i].wait_recv()
-    mine = emball_s.at[:, my_rows, my_half]
-    emb_x = remote(mine, mine, half_sem.at[6], half_sem.at[7], device_at(c, 1 - x, y, z))
-    emb_x.start()
     emb_x.wait_recv()
     mine = emball_s.at[:, :, my_half]
     emb_core = remote(mine, mine, half_sem.at[2], half_sem.at[3], core)
@@ -775,45 +791,70 @@
     def core_copy(p):
         return remote(give_s.at[p], take_s.at[p], core_send.at[p], core_recv.at[p], core)
 
-    def quad_of(t):
-        q = 3 - t // 2
-        qx, qy = lax.rem(x + q // 2, 2), lax.rem(y + lax.rem(q, 2), 2)
-        return qx, qy, qx * 4 + qy * 2 + lax.rem(t, 2)
-
-    def give(t):
-        p = quad_of(t)[2]
+    def pair_of(q, n):
+        return lax.rem(x + q // 2, 2) * 4 + lax.rem(y + q % 2, 2) * 2 + n
+
+    def give(q, n):
+        p = pair_of(q, n)
         give_s[p] = product((1 - c) * 16 + 2 * p)
         core_copy(p).start()
 
-    def keep(t):
-        p = quad_of(t)[2]
+    def keep(q, n):
+        p = pair_of(q, n)
         got = product(c * 16 + 2 * p)
         core_copy(p).wait_recv()
         return got + take_s[p]
 
-    gap = vocab // GRAD_CHUNKS
-
-    def quad_copy(t, chunk):
-        qx, qy, _ = quad_of(t)
-        at = chunk * 6 + t
-        ref = t, pl.ds(chunk * gap, gap)
-        return remote(pass_s.at[ref], came_s.at[ref], quad_send.at[at], quad_recv.at[at], device_at(c, qx, qy, z))
-
-    def pass_on(t):
-        pass_s[t] = keep(t).astype(BF16)
-        for chunk in range(GRAD_CHUNKS):
-            quad_copy(t, chunk).start()
-
-    def forward(t, carry):
-        pass_on(t)
-        give(t + 2)
-        return carry
-
-    give(jnp.int32(0))
-    give(jnp.int32(1))
-    lax.fori_loop(0, 6, forward, 0)
-    own_s[0] = keep(jnp.int32(6))
-    own_s[1] = keep(jnp.int32(7))
+    gap = vocab // 2
+    over_x, over_y = device_at(c, 1 - x, y, z), device_at(c, x, 1 - y, z)
+
+    def quad_copy(q, n, part):
+        at = (3 - q) * 2 + n
+        ref = at, pl.ds(part * gap, gap)
+        to = over_x if q == 2 or (q == 3 and part == 0) else over_y
+        return remote(pass_s.at[ref], came_s.at[ref], quad_send.at[at * 2 + part], quad_recv.at[at * 2 + part], to)
+
+    parts = [slice(0, gap), slice(gap, 2 * gap)]
+    def across(n):
+        pass_s[n] = keep(3, n).astype(BF16)
+        quad_copy(3, n, 0).start()
+        quad_copy(3, n, 1).start()
+
+    def beside(q, n):
+        got = keep(q, n)
+        plain = 2 - q
+        pass_s[(3 - q) * 2 + n, parts[plain]] = got[parts[plain]].astype(BF16)
+        quad_copy(q, n, plain).start()
+        hold_s[2 - q, n] = got[parts[1 - plain]]
+
+    def mixed(q, n):
+        part = q - 1
+        quad_copy(3, n, part).wait_recv()
+        pass_s[(3 - q) * 2 + n, parts[part]] = (
+            hold_s[2 - q, n] + came_s[n, parts[part]].astype(F32)
+        ).astype(BF16)
+        quad_copy(q, n, part).start()
+
+    give(3, 0)
+    give(3, 1)
+    give(2, 0)
+    give(1, 0)
+    across(0)
+    across(1)
+    beside(2, 0)
+    beside(1, 0)
+    give(2, 1)
+    give(1, 1)
+    mixed(1, 0)
+    mixed(2, 0)
+    give(0, 0)
+    beside(2, 1)
+    beside(1, 1)
+    mixed(1, 1)
+    mixed(2, 1)
+    give(0, 1)
+    own_s[0] = keep(0, 0)
+    own_s[1] = keep(0, 1)
 
     pool()
     blocks_out = pltpu.make_async_copy(blocks_s, blocks_ref, local_sem.at[0])
@@ -844,12 +885,11 @@
 
     def to_line(chunk):
         part = slice(chunk * gap, (chunk + 1) * gap)
-        for t in range(6):
-            quad_copy(jnp.int32(t), chunk).wait_recv()
+        for q in (2, 1):
+            for n in range(2):
+                quad_copy(q, n, chunk).wait_recv()
         for t in range(2):
-            total = own_s[t, part]
-            for q in range(1, 4):
-                total = total + came_s[6 - 2 * q + t, part].astype(F32)
+            total = own_s[t, part] + (came_s[2 + t, part].astype(F32) + came_s[4 + t, part].astype(F32))
             for j in range(2):
                 zown_s[2 * t + j, part] = total[:, j * 128 : (j + 1) * 128]
                 zgive_s[2 * t + j, part] = total[:, j * 128 : (j + 1) * 128].astype(BF16)
@@ -914,8 +954,9 @@
     for p in range(8):
         core_copy(p).wait_send()
     for chunk in range(GRAD_CHUNKS):
-        for t in range(6):
-            quad_copy(jnp.int32(t), chunk).wait_send()
+        for q in (3, 2, 1):
+            for n in range(2):
+                quad_copy(q, n, chunk).wait_send()
     for copy in out_copies + [blocks_out]:
         copy.wait()
 
@@ -1021,6 +1062,7 @@
             pltpu.VMEM((8, vocab, 256), F32),
             pltpu.VMEM((8, vocab, 256), F32),
             pltpu.VMEM((2, vocab, 256), F32),
+            pltpu.VMEM((2, 2, vocab // 2, 256), F32),
             pltpu.VMEM((6, vocab, 256), BF16),
             pltpu.VMEM((6, vocab, 256), BF16),
             pltpu.VMEM((4, vocab, 128), BF16),
@@ -1037,8 +1079,8 @@
             dma((2, 11 * max(TABLE_CHUNKS, GRAD_CHUNKS))),
             dma((8,)),
             dma((8,)),
-            dma((6 * GRAD_CHUNKS,)),
-            dma((6 * GRAD_CHUNKS,)),
+            dma((12,)),
+            dma((12,)),
             dma((3 * GRAD_CHUNKS,)),
             dma((3 * GRAD_CHUNKS,)),
             dma((7,)),

time: 88.9 us -> 88.4 us (level)
  no operation moved by 1% of the time
where the time goes in v5:
time: 88.4 us; the launch traced here: 88.2 us
  Pallas kernels  86.8 us (98%)
  between operations  1.45 us (2%)
    pallas_call x1, Pallas kernels, step_shards(): pl.pallas_call(functools.partial(step_kernel, dims), out_shape=(jax.Shape...  82.5 us
    pallas_call x1, Pallas kernels, step_shards(): pl.pallas_call(functools.partial(last_kernel, dims), out_shape=(jax.Shape...  4.29 us

profile of v5, /device:TPU:1, one launch (start us, length us, event | category | flops | bytes accessed | tf_op | source)
XLA Modules:
  0.0 88.2 jit_solution(3511195515593240280)
XLA Ops:
  1.3 82.5 %step.1 = (bf16[2,512,768]{2,1,0:T(8,128)(2,1)}, bf16[2,2,2,4,256,128]{5,4,3,2,1,0:T(8,128)(2,1)}, f32[8,768]{1,0:T(8,128)}) custom-call(s32[2,8]{1,0:T(2,128)} %len_in.1, f32[1,1]{1,0:T(1,128)} %bitcast.8.aux_in, s32[2,1024]{1,0:T(2,128)} %ids_in.1, s32[2,1024]{1,0:T(2,128)} %mask_in.1, bf16[96,256]{1,0:T(8,128)(2,1)} %bitcast.9, ...), custom_call_target="tpu_custom_call" | custom-call | tf_op jit(solution)/shard_map/step/pallas_call | solution.py:1039
  83.8 4.3 %last.1 = (bf16[2,512,768]{2,1,0:T(8,128)(2,1)}, f32[1,1]{1,0:T(1,128)}, f32[96,256]{1,0:T(8,128)}, f32[5,96,768]{2,1,0:T(8,128)}, f32[1,96]{1,0:T(1,128)}, /*index=5*/f32[1,96]{1,0:T(1,128)}) custom-call(bf16[2,512,768]{2,1,0:T(8,128)(2,1)} %get-tuple-element.15.blocks_ref, bf16[2,2,2,4,256,128]{5,4,3,2,1,0:T(8,128)(2,1)} %get-tuple-element.16.final_ref, ...), custom_call_target="tpu_custom_call" | custom-call | tf_op jit(solution)/shard_map/last/pallas_call | solution.py:1112

commit v6 on v5

--- a/solution.py
+++ b/solution.py
@@ -857,7 +857,7 @@
     own_s[1] = keep(0, 1)
 
     pool()
-    blocks_out = pltpu.make_async_copy(blocks_s, blocks_ref, local_sem.at[0])
+    blocks_out = pltpu.make_async_copy(blocks_s, blocks_ref, local_sem.at[4])
     blocks_out.start()
     sums_s[0] = part_s[...]
     sum_copies = [remote(sums_s.at[0], sumr_s.at[0], sum_send.at[0], sum_recv.at[0], core)]
@@ -916,10 +916,11 @@
         final_s[c, x, y, z, part] = total.astype(BF16)
         grads.along_z(chunk)
 
-    def put(chunk):
+    def put(chunk, side):
         part = pl.ds(chunk * gap, gap)
-        ref = ALL, ALL, ALL, ALL, part
-        out_copies.append(pltpu.make_async_copy(final_s.at[ref], final_ref.at[ref], local_sem.at[1 + chunk]))
+        ref = side, ALL, ALL, ALL, part
+        at = local_sem.at[2 * chunk + (0 if side is c else 1)]
+        out_copies.append(pltpu.make_async_copy(final_s.at[ref], final_ref.at[ref], at))
         out_copies[-1].start()
 
     out_copies = []
@@ -934,11 +935,13 @@
     grads.across(0, 1)
     grads.across(1, 1)
     grads.across(0, 2)
+    put(0, c)
     grads.across(1, 2)
+    put(1, c)
     grads.arrived(0)
-    put(0)
+    put(0, 1 - c)
     grads.arrived(1)
-    put(1)
+    put(1, 1 - c)
     grads.drain()
 
     for i in range(4, 7):

time: 88.4 us -> 88.2 us (level)
  no operation moved by 1% of the time
where the time goes in v6:
time: 88.2 us; the launch traced here: 88.1 us
  Pallas kernels  86.6 us (98%)
  between operations  1.45 us (2%)
    pallas_call x1, Pallas kernels, step_shards(): pl.pallas_call(functools.partial(step_kernel, dims), out_shape=(jax.Shape...  82.3 us
    pallas_call x1, Pallas kernels, step_shards(): pl.pallas_call(functools.partial(last_kernel, dims), out_shape=(jax.Shape...  4.29 us

profile of v6, /device:TPU:1, one launch (start us, length us, event | category | flops | bytes accessed | tf_op | source)
XLA Modules:
  0.0 88.1 jit_solution(18422562614843064702)
XLA Ops:
  1.3 82.3 %step.1 = (bf16[2,512,768]{2,1,0:T(8,128)(2,1)}, bf16[2,2,2,4,256,128]{5,4,3,2,1,0:T(8,128)(2,1)}, f32[8,768]{1,0:T(8,128)}) custom-call(s32[2,8]{1,0:T(2,128)} %len_in.1, f32[1,1]{1,0:T(1,128)} %bitcast.8.aux_in, s32[2,1024]{1,0:T(2,128)} %ids_in.1, s32[2,1024]{1,0:T(2,128)} %mask_in.1, bf16[96,256]{1,0:T(8,128)(2,1)} %bitcast.9, ...), custom_call_target="tpu_custom_call" | custom-call | tf_op jit(solution)/shard_map/step/pallas_call | solution.py:1042
  83.6 4.3 %last.1 = (bf16[2,512,768]{2,1,0:T(8,128)(2,1)}, f32[1,1]{1,0:T(1,128)}, f32[96,256]{1,0:T(8,128)}, f32[5,96,768]{2,1,0:T(8,128)}, f32[1,96]{1,0:T(1,128)}, /*index=5*/f32[1,96]{1,0:T(1,128)}) custom-call(bf16[2,512,768]{2,1,0:T(8,128)(2,1)} %get-tuple-element.15.blocks_ref, bf16[2,2,2,4,256,128]{5,4,3,2,1,0:T(8,128)(2,1)} %get-tuple-element.16.final_ref, ...), custom_call_target="tpu_custom_call" | custom-call | tf_op jit(solution)/shard_map/last/pallas_call | solution.py:1115
